TPU v7x, 32 devices: a whole 2x2x4 slice. The times are simulated.
32 devices in a mesh: groups: 2 (over x), seq: 8 (over z, y), exp: 2 (over core).
Axes of the slice: x: 2, y: 2, z: 4, core: 2. Of those that a mesh axis runs over, the one named last changes fastest.
Arguments:
- stream: bfloat16 [2048, 2048], P(('groups', 'seq', 'exp')), parts along dimension 0, may hold values from -5 to 5
- queries: bfloat16 [2048, 4096], P(('groups', 'seq'), 'exp'), parts along dimension 0, may hold values from -131 to 131
- key_rows: bfloat16 [2048, 512], P(('groups', 'seq'), 'exp'), parts along dimension 0, may hold values from -4 to 4
- value_rows: bfloat16 [2048, 512], P(('groups', 'seq'), 'exp'), parts along dimension 0, may hold values from -4 to 4
- out_weight: bfloat16 [2048, 4096], P('seq', 'exp'), may hold values from -0.375 to 0.375
- norm_gain: float32 [2048], replicated, may hold values from 0.1 to 1.9
- expert_ids: int32 [2048, 8], P(('groups', 'seq', 'exp')), parts along dimension 0, may hold values from 0 to 63, all different within a row; in each aligned block of 64 rows (0 to 63, 64 to 127, ...) at most 12 rows name the same one
- gate_weights: float32 [2048, 8], P(('groups', 'seq', 'exp')), parts along dimension 0, may hold values from 0.05 to 0.5
- expert_in: bfloat16 [64, 2048, 1536], P(('seq', 'exp')), may hold values from -0.125 to 0.125
- expert_out: bfloat16 [64, 768, 2048], P(('seq', 'exp')), may hold values from -0.21875 to 0.21875
Outputs:
- layer_out: bfloat16 [2048, 2048], P(('groups', 'seq', 'exp')), parts along dimension 0
There are 2 independent parts, one for each index of `groups`. A program takes and returns all parts, laid end to end along the dimension named above; an argument that names none is the same for every part. Nothing has to cross between parts.
Inputs may be any that keep to these rules, and one draw needn't show every extreme that they name: `expert_ids`: each row names 8 different experts. Among the 64 rows of one device (aligned blocks of rows), no expert is named more than 12 times, a bound that some block reaches.
All inputs are finite; a program needn't handle non-finite values.
Results may differ from a plain program's by a relative error of at most 0.0095.
Values may be sent and summed in bfloat16 or wider, within the bound.
A program may use at most 128 MiB of HBM per device.

v0:
```python
import functools

import jax
import jax.numpy as jnp
from jax import lax
from jax.experimental import pallas as pl
from jax.experimental.pallas import tpu as pltpu
from jax.sharding import PartitionSpec as P

HD = 128
EXPERTS = 64
CAP = 12
LOW = 2
PARTS = 4
VMEM_LIMIT = 67043328
neg_large = -1e30


def split_position():
    seq = lax.axis_index("seq")
    return seq // LOW, seq % LOW, lax.axis_index("exp")


def line_barrier(high, h, l, e):
    barrier = pltpu.get_barrier_semaphore()

    def greet(target):
        pl.semaphore_signal(barrier, inc=1, device_id=target, device_id_type=pl.DeviceIdType.MESH)

    @pl.when(h + 1 < high)
    def _():
        greet({"seq": (h + 1) * LOW + l})

    @pl.when(h > 0)
    def _():
        greet({"seq": (h - 1) * LOW + l})

    greet({"seq": h * LOW + 1 - l})
    greet({"exp": 1 - e})

    ends = jnp.where(h + 1 < high, 1, 0) + jnp.where(h > 0, 1, 0)
    pl.semaphore_wait(barrier, ends + 2)


def gather_steps(high, outs, cross, parts, recv, send, h, l, e, beside=None):
    count = len(outs)

    def slot(a, h0, l0, e0, c):
        rows = outs[a].shape[-2] // parts[a]
        at = (h0, l0, e0) if cross[a] else (h0, l0)
        return outs[a].at[at + (pl.ds(c * rows, rows),)]

    def copy(a, h0, l0, e0, c, way):
        target = (
            {"seq": (h + 1) * LOW + l},
            {"seq": (h - 1) * LOW + l},
            {"seq": h * LOW + 1 - l},
            {"exp": 1 - e},
        )[way]
        ref = slot(a, h0, l0, e0, c)
        return pltpu.make_async_remote_copy(
            src_ref=ref,
            dst_ref=ref,
            send_sem=send[a].at[way, h0, l0, c],
            recv_sem=recv[a].at[h0, l0, e0, c],
            device_id=target,
            device_id_type=pl.DeviceIdType.MESH,
        )

    def pass_on(a, h0, c, right, left):
        if right:
            @pl.when(h + 1 < high)
            def _():
                copy(a, h0, l, e, c, 0).start()
        if left:
            @pl.when(h > 0)
            def _():
                copy(a, h0, l, e, c, 1).start()
        copy(a, h0, l, e, c, 2).start()
        if cross[a]:
            copy(a, h0, l, e, c, 3).start()

    def from_across(a, h0, c):
        copy(a, h0, 1 - l, e, c, 2).wait_recv()
        if cross[a]:
            copy(a, h0, 1 - l, e, c, 3).start()

    for a in range(count):
        for c in range(parts[a]):
            pass_on(a, h, c, True, True)
    if beside is not None:
        beside(0)
    for t in range(1, high + 1):
        if t < high:
            for a in range(count):
                for c in range(parts[a]):
                    @pl.when(h - t >= 0)
                    def _():
                        copy(a, h - t, l, e, c, 0).wait_recv()
                        pass_on(a, h - t, c, True, False)

                    @pl.when(h + t < high)
                    def _():
                        copy(a, h + t, l, e, c, 1).wait_recv()
                        pass_on(a, h + t, c, False, True)
        for a in range(count):
            for c in range(parts[a]):
                if t == 1:
                    from_across(a, h, c)
                else:
                    @pl.when(h - t + 1 >= 0)
                    def _():
                        from_across(a, h - t + 1, c)

                    @pl.when(h + t - 1 < high)
                    def _():
                        from_across(a, h + t - 1, c)
        if beside is not None and t < high:
            beside(t)
    for a in range(count):
        for c in range(parts[a]):
            for h0 in range(high):
                if cross[a]:
                    for l0 in range(LOW):
                        copy(a, h0, l0, 1 - e, c, 3).wait_recv()
                        copy(a, h0, l0, e, c, 3).wait_send()
                copy(a, h0, l, e, c, 2).wait_send()

                @pl.when((h + 1 < high) & (h0 <= h))
                def _():
                    copy(a, h0, l, e, c, 0).wait_send()

                @pl.when((h > 0) & (h0 >= h))
                def _():
                    copy(a, h0, l, e, c, 1).wait_send()


def all_barrier(high, h, l, e):
    barrier = pltpu.get_barrier_semaphore()
    mesh_id = pl.DeviceIdType.MESH
    for d in range(1, high):
        pl.semaphore_signal(
            barrier, inc=1, device_id={"seq": (h + d) % high * LOW + l}, device_id_type=mesh_id
        )
    pl.semaphore_signal(barrier, inc=1, device_id={"seq": h * LOW + 1 - l}, device_id_type=mesh_id)
    pl.semaphore_signal(barrier, inc=1, device_id={"exp": 1 - e}, device_id_type=mesh_id)
    pl.semaphore_wait(barrier, high + 1)


def attend(query_ref, kv_ref, out_ref, me, done):
    half = kv_ref.shape[-1] // 2
    groups = half // HD
    rows, columns = query_ref.shape
    per_group = columns // (groups * HD)
    scale = 1.0 / (HD ** 0.5)
    stacked = per_group * rows
    for g in range(groups):
        q = jnp.concatenate(
            [query_ref[:, pl.ds((g * per_group + i) * HD, HD)] for i in range(per_group)], axis=0
        )

        def piece(b, state, masked):
            largest, total, summed = state
            k = kv_ref[b // LOW, b % LOW, :, pl.ds(g * HD, HD)]
            v = kv_ref[b // LOW, b % LOW, :, pl.ds(half + g * HD, HD)]
            scores = lax.dot_general(
                q, k, (((1,), (1,)), ((), ())), preferred_element_type=jnp.float32
            ) * scale
            if masked:
                row = lax.broadcasted_iota(jnp.int32, scores.shape, 0) % rows
                column = lax.broadcasted_iota(jnp.int32, scores.shape, 1)
                scores = jnp.where(column <= row, scores, neg_large)
            new = jnp.maximum(largest, jnp.max(scores, axis=-1, keepdims=True))
            rescale = jnp.exp(largest - new)
            exps = jnp.exp(scores - new)
            total = total * rescale + jnp.sum(exps, axis=-1, keepdims=True)
            summed = summed * rescale + jnp.dot(
                exps.astype(jnp.bfloat16), v, preferred_element_type=jnp.float32
            )
            return new, total, summed

        state = (
            jnp.full((stacked, 1), neg_large, jnp.float32),
            jnp.zeros((stacked, 1), jnp.float32),
            jnp.zeros((stacked, HD), jnp.float32),
        )
        state = piece(me, state, True)
        state = lax.fori_loop(0, me, lambda b, s: piece(b, s, False), state)
        result = (state[2] / state[1]).astype(out_ref.dtype)
        for i in range(per_group):
            out_ref[:, pl.ds((g * per_group + i) * HD, HD)] = result[i * rows : (i + 1) * rows]
        done(g)


def front_kernel(
    high, key_in, value_in, ids_ref, gates_ref, query_ref, weight_in, stream_ref, gain_ref,
    mixed_ref, normed_ref, meta_all,
    kv_all, weights, context, contexts, part, mine, ready, landed,
    kv_r, meta_r, kv_s, meta_s, local, weight_sem, line_s, line_r, over_s, over_r, away_s, away_r
):
    h, l, e = split_position()
    mesh_id = pl.DeviceIdType.MESH
    half = key_in.shape[1]
    top = ids_ref.shape[1]
    copies = [
        pltpu.make_async_copy(key_in, kv_all.at[h, l, :, pl.ds(0, half)], local.at[0]),
        pltpu.make_async_copy(value_in, kv_all.at[h, l, :, pl.ds(half, half)], local.at[1]),
        pltpu.make_async_copy(weight_in, weights.at[l], local.at[2]),
    ]
    for one in copies:
        one.start()
    meta_all[h, l, e] = jnp.zeros_like(meta_all[h, l, e])
    meta_all[h, l, e, :, pl.ds(0, top)] = ids_ref[...].astype(jnp.float32)
    meta_all[h, l, e, :, pl.ds(top, top)] = gates_ref[...]
    all_barrier(high, h, l, e)
    for one in copies:
        one.wait()
    gather_steps(
        high, (kv_all, meta_all), (False, True), (2, 1), (kv_r, meta_r), (kv_s, meta_s), h, l, e
    )
    weight_copy = pltpu.make_async_remote_copy(
        src_ref=weights.at[l],
        dst_ref=weights.at[l],
        send_sem=weight_sem.at[0],
        recv_sem=weight_sem.at[1],
        device_id={"seq": h * LOW + 1 - l},
        device_id_type=mesh_id,
    )
    weight_copy.start()
    parts = half // HD
    columns = context.shape[1] // parts

    def hop(way, h0, c):
        ref = contexts.at[h0, :, pl.ds(c * columns, columns)]
        return pltpu.make_async_remote_copy(
            src_ref=ref,
            dst_ref=ref,
            send_sem=line_s.at[way, h0, c],
            recv_sem=line_r.at[h0, c],
            device_id={"seq": (h + 1 - 2 * way) * LOW + l},
            device_id_type=mesh_id,
        )

    def hops(h0, c, right, left):
        if right:
            @pl.when(h + 1 < high)
            def _():
                hop(0, h0, c).start()
        if left:
            @pl.when(h > 0)
            def _():
                hop(1, h0, c).start()

    def done(c):
        at = pl.ds(c * columns, columns)
        own = pltpu.make_async_copy(context.at[:, at], contexts.at[h, :, at], local.at[0])
        own.start()
        own.wait()
        hops(h, c, True, True)

    attend(query_ref, kv_all, context, h * LOW + l, done)
    for t in range(1, high):
        for c in range(parts):
            @pl.when(h - t >= 0)
            def _():
                hop(0, h - t, c).wait_recv()
                hops(h - t, c, True, False)

            @pl.when(h + t < high)
            def _():
                hop(1, h + t, c).wait_recv()
                hops(h + t, c, False, True)
    weight_back = pltpu.make_async_remote_copy(
        src_ref=weights.at[1 - l],
        dst_ref=weights.at[1 - l],
        send_sem=weight_sem.at[0],
        recv_sem=weight_sem.at[1],
        device_id={"seq": h * LOW + 1 - l},
        device_id_type=mesh_id,
    )
    weight_back.wait_recv()
    rows_e, features = part.shape[2:]
    slim = features // LOW

    def over(h0):
        return pltpu.make_async_remote_copy(
            src_ref=part.at[h0, 1 - e],
            dst_ref=mine.at[h0],
            send_sem=over_s.at[h0],
            recv_sem=over_r.at[h0],
            device_id={"exp": 1 - e},
            device_id_type=mesh_id,
        )

    def away(h0, source):
        return pltpu.make_async_remote_copy(
            src_ref=ready.at[h0],
            dst_ref=landed.at[source],
            send_sem=away_s.at[h0],
            recv_sem=away_r.at[source],
            device_id={"seq": h0 * LOW + l},
            device_id_type=mesh_id,
        )

    @pl.loop(0, high)
    def _(d):
        h0 = (h + 1 + d) % high
        for l0 in range(LOW):
            product = lax.dot_general(
                contexts[h0], weights[l0], (((1,), (1,)), ((), ())), preferred_element_type=jnp.float32
            ).astype(part.dtype)
            for e0 in range(2):
                part[h0, e0, :, pl.ds(l0 * slim, slim)] = product[e0 * rows_e : (e0 + 1) * rows_e]
        over(h0).start()

    for d in range(1, high + 1):
        h0 = (h + d) % high
        over(h0).wait_recv()
        total = part[h0, e].astype(jnp.float32) + mine[h0].astype(jnp.float32)
        ready[h0] = total.astype(ready.dtype)
        if d < high:
            away(h0, h).start()
    landed[h] = ready[h]
    for d in range(1, high):
        away((h + d) % high, (h + high - d) % high).wait_recv()
    squares = None
    for h0 in range(high):
        block = pl.ds(h0 * features, features)
        value = stream_ref[:, block].astype(jnp.float32) + landed[h0].astype(jnp.float32)
        mixed_ref[:, block] = value
        term = jnp.sum(value * value, axis=-1, keepdims=True)
        squares = term if squares is None else squares + term
    factor = lax.rsqrt(squares / (high * features) + 1e-06)
    for h0 in range(high):
        block = pl.ds(h0 * features, features)
        normed_ref[:, block] = (mixed_ref[:, block] * factor * gain_ref[:, block]).astype(
            normed_ref.dtype
        )
    weight_copy.wait_send()
    for h0 in range(high):
        over(h0).wait_send()
        for c in range(parts):
            @pl.when((h + 1 < high) & (h0 <= h))
            def _():
                hop(0, h0, c).wait_send()

            @pl.when((h > 0) & (h0 >= h))
            def _():
                hop(1, h0, c).wait_send()
    for d in range(1, high):
        away((h + d) % high, h).wait_send()


def front(keys, values, ids, gates, queries, weight, stream, gain, high):
    whole = pl.BlockSpec(memory_space=pltpu.VMEM)
    span = queries.shape[0]
    rows = stream.shape[0]
    features = weight.shape[0] * LOW
    kind = jnp.bfloat16
    sem = pltpu.SemaphoreType.DMA
    return pl.pallas_call(
        functools.partial(front_kernel, high),
        out_shape=(
            jax.ShapeDtypeStruct(stream.shape, jnp.float32),
            jax.ShapeDtypeStruct(stream.shape, kind),
            jax.ShapeDtypeStruct((high, LOW, 2, rows, 128), jnp.float32),
        ),
        in_specs=[whole] * 8,
        out_specs=(whole,) * 3,
        scratch_shapes=[
            pltpu.VMEM((high, LOW, span, 2 * keys.shape[1]), kind),
            pltpu.VMEM((LOW,) + weight.shape, kind),
            pltpu.VMEM(queries.shape, kind),
            pltpu.VMEM((high,) + queries.shape, kind),
            pltpu.VMEM((high, 2, rows, features), kind),
            pltpu.VMEM((high, rows, features), kind),
            pltpu.VMEM((high, rows, features), kind),
            pltpu.VMEM((high, rows, features), kind),
            sem((high, LOW, 2, 2)),
            sem((high, LOW, 2, 1)),
            sem((4, high, LOW, 2)),
            sem((4, high, LOW, 1)),
            sem((3,)),
            sem((2,)),
            sem((2, high, keys.shape[1] // HD)),
            sem((high, keys.shape[1] // HD)),
            sem((high,)),
            sem((high,)),
            sem((high,)),
            sem((high,)),
        ],
        compiler_params=pltpu.CompilerParams(
            collective_id=1, has_side_effects=True, vmem_limit_bytes=VMEM_LIMIT
        ),
        name="front",
    )(keys, values, ids, gates, queries, weight, stream, gain)


def back_kernel(
    high, parts, top, normed_ref, mixed_ref, meta_ref, first_hbm, second_hbm, out_ref,
    choose_ref, combine_ref, every, first, second, picked, act, near, sums, across, running, line,
    local, weight_sem, recv, send, near_s, near_r, across_s, across_r, line_s, line_r
):
    h, l, e = split_position()
    experts, width, double = first.shape
    hidden = double // 2
    slots = picked.shape[2]
    loads = []
    for i in range(experts):
        loads.append(pltpu.make_async_copy(first_hbm.at[i], first.at[i], weight_sem.at[0, i]))
        loads.append(pltpu.make_async_copy(second_hbm.at[i], second.at[i], weight_sem.at[1, i]))
    for one in loads:
        one.start()
    own = pltpu.make_async_copy(normed_ref, every.at[h, l, e], local.at[0])
    own.start()
    line_barrier(high, h, l, e)
    own.wait()
    device = (h * LOW + l) * 2 + e
    tokens_here, total = combine_ref.shape[1:]
    span = every.shape[3]

    def build(h0):
        meta = meta_ref[h0].reshape(tokens_here, 128)
        moved = pltpu.roll(meta, 128 - top, axis=1)
        lane = lax.broadcasted_iota(jnp.int32, meta.shape, 1)
        chosen, gates, table = [], [], jnp.zeros_like(meta)
        for i in range(experts):
            here = (device * experts + i).astype(jnp.float32)
            hit = (meta == here) & (lane < top)
            chosen.append(jnp.sum(jnp.where(hit, 1.0, 0.0), axis=1, keepdims=True))
            gates.append(jnp.sum(jnp.where(hit, moved, 0.0), axis=1, keepdims=True))
            table = table + jnp.where(lane == i, chosen[i], 0.0)
        square = (tokens_here, tokens_here)
        row = lax.broadcasted_iota(jnp.int32, square, 0)
        column = lax.broadcasted_iota(jnp.int32, square, 1)
        earlier = jnp.where((column < row) & (row // span == column // span), 1.0, 0.0)
        place = jnp.dot(
            earlier.astype(jnp.bfloat16), table.astype(jnp.bfloat16), preferred_element_type=jnp.float32
        )
        wide = (tokens_here, -(-total // 128) * 128)
        number = lax.broadcasted_iota(jnp.int32, wide, 1).astype(jnp.float32)
        block = (lax.broadcasted_iota(jnp.int32, (tokens_here, 1), 0) // span).astype(jnp.float32)
        onehot, weigh = jnp.zeros(wide, jnp.float32), jnp.zeros(wide, jnp.float32)
        for i in range(experts):
            within = jnp.sum(jnp.where(lane == i, place, 0.0), axis=1, keepdims=True)
            match = (number == within + block * CAP + i * slots) & (chosen[i] > 0.5)
            onehot = onehot + jnp.where(match, 1.0, 0.0)
            weigh = weigh + jnp.where(match, gates[i], 0.0)
        combine_ref[h0] = weigh[:, :total].astype(combine_ref.dtype)
        choose_ref[h0] = jnp.transpose(onehot)[:total].astype(choose_ref.dtype)

    gather_steps(high, (every,), (True,), (parts,), (recv,), (send,), h, l, e, build)
    for one in loads:
        one.wait()
    rows_all = every.shape[1] * every.shape[2] * every.shape[3]
    tile = 512

    @pl.loop(0, high)
    def _(h0):
        for n in range(0, width, tile):
            tokens = every[h0, :, :, :, pl.ds(n, tile)].reshape(rows_all, tile)
            value = jnp.dot(choose_ref[h0], tokens, preferred_element_type=jnp.float32)
            for i in range(experts):
                picked[i, h0, :, pl.ds(n, tile)] = value[i * slots : (i + 1) * slots].astype(
                    picked.dtype
                )

    def run(i, carry):
        step = 256
        rows = picked[i].reshape(high * slots, width)
        for f in range(0, hidden, step):
            gate = jnp.dot(rows, first[i, :, pl.ds(f, step)], preferred_element_type=jnp.float32)
            up = jnp.dot(
                rows, first[i, :, pl.ds(hidden + f, step)], preferred_element_type=jnp.float32
            )
            act[:, pl.ds(f, step)] = (gate / (1.0 + jnp.exp(-gate)) * up).astype(act.dtype)
        for n in range(0, width, tile):
            value = jnp.dot(
                act[...], second[i, :, pl.ds(n, tile)], preferred_element_type=jnp.float32
            ).astype(picked.dtype)
            picked[i, :, :, pl.ds(n, tile)] = value.reshape(high, slots, tile)
        return carry

    lax.fori_loop(0, experts, run, 0)
    scatter_steps(
        high, parts, every, mixed_ref, out_ref, near, sums, across, running, line,
        near_s, near_r, across_s, across_r, line_s, line_r, h, l, e, combine_ref, picked, tile
    )


def scatter_steps(
    high, parts, part_ref, mixed_ref, out_ref, near, sums, across, running, line,
    near_s, near_r, across_s, across_r, line_s, line_r, h, l, e, combine_ref, picked, tile
):
    rows = part_ref.shape[-2] // parts
    mesh_id = pl.DeviceIdType.MESH
    order = []
    for i in range(high):
        order.append(i // 2 if i % 2 == 0 else high - 1 - i // 2)

    def to_near(h0, l0, c):
        at = pl.ds(c * rows, rows)
        return pltpu.make_async_remote_copy(
            src_ref=part_ref.at[h0, l0, 1 - e, at],
            dst_ref=near.at[h0, l0, at],
            send_sem=near_s.at[h0, l0, c],
            recv_sem=near_r.at[h0, l0, c],
            device_id={"exp": 1 - e},
            device_id_type=mesh_id,
        )

    def to_across(h0, c):
        at = pl.ds(c * rows, rows)
        return pltpu.make_async_remote_copy(
            src_ref=sums.at[h0, at],
            dst_ref=across.at[h0, at],
            send_sem=across_s.at[h0, c],
            recv_sem=across_r.at[h0, c],
            device_id={"seq": h * LOW + 1 - l},
            device_id_type=mesh_id,
        )

    def to_line(way, h0, c):
        at = pl.ds(c * rows, rows)
        return pltpu.make_async_remote_copy(
            src_ref=running.at[h0, at],
            dst_ref=line.at[way, h0, at],
            send_sem=line_s.at[way, h0, c],
            recv_sem=line_r.at[way, h0, c],
            device_id={"seq": (h - 1 + 2 * way) * LOW + l},
            device_id_type=mesh_id,
        )

    pieces = [(h0, c) for h0 in order for c in range(parts)]
    experts, width = picked.shape[0], picked.shape[-1]
    shape = part_ref.shape[1:4]
    for h0 in order:
        for n in range(0, width, tile):
            rows_here = jnp.concatenate(
                [picked[i, h0, :, pl.ds(n, tile)] for i in range(experts)], axis=0
            )
            value = jnp.dot(combine_ref[h0], rows_here, preferred_element_type=jnp.float32)
            part_ref[h0, :, :, :, pl.ds(n, tile)] = value.astype(part_ref.dtype).reshape(
                shape + (tile,)
            )
        for c in range(parts):
            to_near(h0, 1 - l, c).start()
        for c in range(parts):
            to_near(h0, l, c).start()
    for h0, c in pieces:
        at = pl.ds(c * rows, rows)
        to_near(h0, 1 - l, c).wait_recv()
        value = part_ref[h0, 1 - l, e, at].astype(jnp.float32) + near[h0, 1 - l, at].astype(jnp.float32)
        sums[h0, at] = value.astype(sums.dtype)
        to_across(h0, c).start()
    for h0, c in pieces:
        at = pl.ds(c * rows, rows)
        to_near(h0, l, c).wait_recv()
        to_across(h0, c).wait_recv()

        def held():
            value = part_ref[h0, l, e, at].astype(jnp.float32) + near[h0, l, at].astype(jnp.float32)
            return value + across[h0, at].astype(jnp.float32)

        @pl.when(h0 < h)
        def _():
            @pl.when(h + 1 < high)
            def _():
                to_line(0, h0, c).wait_recv()
                running[h0, at] = (held() + line[0, h0, at].astype(jnp.float32)).astype(running.dtype)

            @pl.when(h + 1 >= high)
            def _():
                running[h0, at] = held().astype(running.dtype)

            to_line(0, h0, c).start()

        @pl.when(h0 > h)
        def _():
            @pl.when(h > 0)
            def _():
                to_line(1, h0, c).wait_recv()
                running[h0, at] = (held() + line[1, h0, at].astype(jnp.float32)).astype(running.dtype)

            @pl.when(h <= 0)
            def _():
                running[h0, at] = held().astype(running.dtype)

            to_line(1, h0, c).start()
    for c in range(parts):
        at = pl.ds(c * rows, rows)
        value = part_ref[h, l, e, at].astype(jnp.float32) + near[h, l, at].astype(jnp.float32)
        value = value + across[h, at].astype(jnp.float32) + mixed_ref[at, :]
        mixed_ref_sum = value

        @pl.when(h + 1 < high)
        def _():
            to_line(0, h, c).wait_recv()

        @pl.when(h + 1 >= high)
        def _():
            line[0, h, at] = jnp.zeros_like(line[0, h, at])

        @pl.when(h > 0)
        def _():
            to_line(1, h, c).wait_recv()

        @pl.when(h <= 0)
        def _():
            line[1, h, at] = jnp.zeros_like(line[1, h, at])

        value = mixed_ref_sum + line[0, h, at].astype(jnp.float32) + line[1, h, at].astype(jnp.float32)
        out_ref[at, :] = value.astype(out_ref.dtype)
    for h0, c in pieces:
        to_near(h0, l, c).wait_send()
        to_near(h0, 1 - l, c).wait_send()
        to_across(h0, c).wait_send()

        @pl.when(h0 < h)
        def _():
            to_line(0, h0, c).wait_send()

        @pl.when(h0 > h)
        def _():
            to_line(1, h0, c).wait_send()


def back(normed, mixed, meta, expert_in, expert_out, high, top):
    rows, width = mixed.shape
    parts = PARTS
    whole = pl.BlockSpec(memory_space=pltpu.VMEM)
    away = pl.BlockSpec(memory_space=pl.ANY)
    kind = jnp.bfloat16
    sem = pltpu.SemaphoreType.DMA
    experts = expert_in.shape[0]
    slots = LOW * 2 * CAP
    tokens = LOW * 2 * rows
    return pl.pallas_call(
        functools.partial(back_kernel, high, parts, top),
        out_shape=jax.ShapeDtypeStruct((rows, width), kind),
        in_specs=[whole] * 3 + [away] * 2,
        out_specs=whole,
        scratch_shapes=[
            pltpu.VMEM((high, experts * slots, tokens), kind),
            pltpu.VMEM((high, tokens, experts * slots), kind),
            pltpu.VMEM((high, LOW, 2, rows, width), kind),
            pltpu.VMEM(expert_in.shape, kind),
            pltpu.VMEM(expert_out.shape, kind),
            pltpu.VMEM((experts, high, slots, width), kind),
            pltpu.VMEM((high * slots, expert_out.shape[1]), kind),
            pltpu.VMEM((high, LOW, rows, width), kind),
            pltpu.VMEM((high, rows, width), kind),
            pltpu.VMEM((high, rows, width), kind),
            pltpu.VMEM((high, rows, width), kind),
            pltpu.VMEM((2, high, rows, width), kind),
            sem((1,)),
            sem((2, experts)),
            sem((high, LOW, 2, parts)),
            sem((4, high, LOW, parts)),
        ]
        + [sem((high, LOW, parts))] * 2
        + [sem((high, parts))] * 2
        + [sem((2, high, parts))] * 2,
        compiler_params=pltpu.CompilerParams(
            collective_id=2, has_side_effects=True, vmem_limit_bytes=VMEM_LIMIT
        ),
        name="back",
    )(normed, mixed, meta, expert_in, expert_out)


def on_device(
    stream,
    queries,
    key_rows,
    value_rows,
    out_weight,
    norm_gain,
    expert_ids,
    gate_weights,
    expert_in,
    expert_out,
):
    high = lax.axis_size("seq") // LOW
    mixed, normed, meta = front(
        key_rows, value_rows, expert_ids, gate_weights, queries, out_weight, stream,
        norm_gain.reshape(1, -1), high,
    )
    return back(normed, mixed, meta, expert_in, expert_out, high, expert_ids.shape[1])


def solution(mesh):
    in_specs = (
        P(("groups", "seq", "exp"), None),
        P(("groups", "seq"), "exp"),
        P(("groups", "seq"), "exp"),
        P(("groups", "seq"), "exp"),
        P("seq", "exp"),
        P(),
        P(("groups", "seq", "exp"), None),
        P(("groups", "seq", "exp"), None),
        P(("seq", "exp"), None, None),
        P(("seq", "exp"), None, None),
    )
    out_specs = P(("groups", "seq", "exp"), None)
    return jax.shard_map(
        on_device, mesh=mesh, in_specs=in_specs, out_specs=out_specs, check_vma=False
    )
```

profile of v0, /device:TPU:9, one launch (start us, length us, event | category | flops | bytes accessed | tf_op | source)
XLA Modules:
  0.0 150.2 jit_solution(4667959628495461863)
XLA Ops:
  0.0 1.4 copy.11.ids_ref
  1.4 1.4 copy.12.gates_ref
  2.8 71.7 %front.1 = (f32[64,2048]{1,0:T(8,128)}, bf16[64,2048]{1,0:T(8,128)(2,1)}, f32[4,2,2,64,128]{4,3,2,1,0:T(8,128)}) custom-call(bf16[128,256]{1,0:T(8,128)(2,1)} %key_in.1, bf16[128,256]{1,0:T(8,128)(2,1)} %value_in.1, s32[64,8]{1,0:T(8,128)} %copy.11.ids_ref, f32[64,8]{1,0:T(8,128)} %copy.12.gates_ref, bf16[128,2048]{1,0:T(8,128)(2,1)} %query_ref.1, ...), custom_call_target="tpu_custom_call" | custom-call | tf_op jit(solution)/shard_map/front/pallas_call | solution.py:361
  74.5 74.0 %back.1 = bf16[64,2048]{1,0:T(8,128)(2,1)} custom-call(bf16[64,2048]{1,0:T(8,128)(2,1)} %get-tuple-element.8.normed_ref, f32[64,2048]{1,0:T(8,128)} %get-tuple-element.9.mixed_ref, f32[4,2,2,64,128]{4,3,2,1,0:T(8,128)} %get-tuple-element.10.meta_ref, bf16[4,2048,1536]{2,1,0:T(8,128)(2,1)} %first_hbm.1, bf16[4,768,2048]{2,1,0:T(8,128)(2,1)} %second_hbm.1), custom_call_target="tpu_custom_call" | custom-call | tf_op jit(solution)/shard_map/back/pallas_call | solution.py:638
  148.5 1.7 %copy.14 = bf16[64,2048]{1,0:T(8,128)(2,1)} copy(bf16[64,2048]{1,0:T(8,128)(2,1)} %back.1) | data formatting | bytes 524288
where the time goes:
time: 152 us; the launch traced here: 150 us
  Pallas kernels  146 us (96%)
  local copies, waits for them, and re-layouts  4.43 us (3%)
    pallas_call x1, Pallas kernels, back(): pl.pallas_call(functools.partial(back_kernel, high, parts, top), out_shap...  74 us
    pallas_call x1, Pallas kernels, front(): pl.pallas_call(functools.partial(front_kernel, high), out_shape=(jax.Shap...  71.7 us
    unnamed x3, local copies, waits for them, and re-layouts  4.43 us

commit v1 on v0

--- a/solution.py
+++ b/solution.py
@@ -135,259 +135,437 @@
                     copy(a, h0, l, e, c, 1).wait_send()
 
 
-def all_barrier(high, h, l, e):
+def whole_barrier(seq, groups):
     barrier = pltpu.get_barrier_semaphore()
+    me, e = lax.axis_index("seq"), lax.axis_index("exp")
+
+    def greet(target):
+        pl.semaphore_signal(barrier, inc=1, device_id=target, device_id_type=pl.DeviceIdType.MESH)
+
+    greet({"exp": 1 - e})
+    for d in range(1, seq):
+        for e0 in range(2):
+            greet({"seq": (me + d) % seq, "exp": e0})
+    count = 2 * seq - 1
+    if groups % 2 == 0:
+        greet({"groups": flip(lax.axis_index("groups"))})
+        count += 1
+    pl.semaphore_wait(barrier, count)
+
+
+def flip(i):
+    return i + 1 - 2 * (i % 2)
+
+
+def attend_piece(q, k, v, state, allowed):
+    largest, total, summed = state
+    scale = 1.0 / (HD ** 0.5)
+    scores = lax.dot_general(
+        q, k, (((1,), (1,)), ((), ())), preferred_element_type=jnp.float32
+    ) * scale
+    if allowed is not None:
+        scores = jnp.where(allowed, scores, neg_large)
+    new = jnp.maximum(largest, jnp.max(scores, axis=-1, keepdims=True))
+    rescale = jnp.exp(largest - new)
+    exps = jnp.exp(scores - new)
+    total = total * rescale + jnp.sum(exps, axis=-1, keepdims=True)
+    summed = summed * rescale + jnp.dot(
+        exps.astype(jnp.bfloat16), v, preferred_element_type=jnp.float32
+    )
+    return new, total, summed
+
+
+def front_kernel(
+    high, groups, chunks, key_in, value_in, ids_ref, gates_ref, query_in, weight_in, stream_in, gain_ref,
+    mixed_ref, normed_ref, meta_all,
+    query_ref, stream_ref, kv, weights, contexts, part, mine, ready, landed,
+    local, meta_s, meta_r, kv_s, kv_r, ctx_s, ctx_r, weight_s, weight_r, swap_s, over_s, over_r,
+    away_s, away_r
+):
+    h, l, e = split_position()
+    q, p = h // 2, h % 2
+    me, seq = h * LOW + l, high * LOW
+    squares = high // 2
+    paired = groups % 2 == 0
+    x = lax.axis_index("groups") % 2 if paired else 0
     mesh_id = pl.DeviceIdType.MESH
-    for d in range(1, high):
-        pl.semaphore_signal(
-            barrier, inc=1, device_id={"seq": (h + d) % high * LOW + l}, device_id_type=mesh_id
-        )
-    pl.semaphore_signal(barrier, inc=1, device_id={"seq": h * LOW + 1 - l}, device_id_type=mesh_id)
-    pl.semaphore_signal(barrier, inc=1, device_id={"exp": 1 - e}, device_id_type=mesh_id)
-    pl.semaphore_wait(barrier, high + 1)
-
-
-def attend(query_ref, kv_ref, out_ref, me, done):
-    half = kv_ref.shape[-1] // 2
-    groups = half // HD
-    rows, columns = query_ref.shape
-    per_group = columns // (groups * HD)
-    scale = 1.0 / (HD ** 0.5)
-    stacked = per_group * rows
-    for g in range(groups):
-        q = jnp.concatenate(
+    heads = key_in.shape[1] // HD
+    span, columns = query_ref.shape
+    per_group = columns // (heads * HD)
+    wide = per_group * HD
+    top, rows_e = ids_ref.shape
+    features = weight_in.shape[0]
+    loads = []
+    for g in range(heads):
+        at = pl.ds(g * HD, HD)
+        loads.append(pltpu.make_async_copy(key_in.at[:, at], kv.at[g, h, l, :, pl.ds(0, HD)], local.at[2 * g]))
+        loads.append(pltpu.make_async_copy(value_in.at[:, at], kv.at[g, h, l, :, pl.ds(HD, HD)], local.at[2 * g + 1]))
+    query_load = pltpu.make_async_copy(query_in, query_ref, local.at[2 * heads])
+    weight_load = pltpu.make_async_copy(weight_in, weights.at[q], local.at[2 * heads + 1])
+    stream_load = pltpu.make_async_copy(stream_in, stream_ref, local.at[2 * heads + 2])
+    for one in loads + [query_load, weight_load, stream_load]:
+        one.start()
+
+    @pl.when(l == 0)
+    def _():
+        for g in range(heads):
+            kv[g, h, 1] = jnp.zeros_like(kv[g, h, 1])
+
+    listed = jnp.concatenate([ids_ref[...].astype(jnp.float32), gates_ref[...]], axis=0)
+    blank = jnp.zeros_like(listed)
+    meta_all[h, l, e] = jnp.where(
+        e == 0,
+        jnp.concatenate([listed, blank], axis=1),
+        jnp.concatenate([blank, listed], axis=1),
+    ).astype(meta_all.dtype)
+    whole_barrier(seq, groups)
+
+    def kv_copy(way, g, h0, l0):
+        ref = kv.at[g, h0, l0]
+        target = ({"seq": (h + 1) * LOW + l}, {"seq": h * LOW + 1 - l})[way]
+        return pltpu.make_async_remote_copy(
+            src_ref=ref,
+            dst_ref=ref,
+            send_sem=kv_s.at[way, g, h0, l0],
+            recv_sem=kv_r.at[g, h0, l0],
+            device_id=target,
+            device_id_type=mesh_id,
+        )
+
+    def meta_copy(d, e0, source):
+        s0 = (me + d) % seq
+        ref = meta_all.at[h, l, e]
+        return pltpu.make_async_remote_copy(
+            src_ref=ref,
+            dst_ref=ref,
+            send_sem=meta_s.at[s0, e0],
+            recv_sem=meta_r.at[source[0], source[1]],
+            device_id={"seq": s0, "exp": e0},
+            device_id_type=mesh_id,
+        )
+
+    def weight_rows(half, c):
+        step = features // (2 * chunks)
+        return pl.ds((half * chunks + c) * step, step)
+
+    def weight_copy(q0, half, c, owner):
+        ref = weights.at[owner, weight_rows(half, c)]
+        return pltpu.make_async_remote_copy(
+            src_ref=ref,
+            dst_ref=ref,
+            send_sem=weight_s.at[q0, half, c],
+            recv_sem=weight_r.at[owner, half, c],
+            device_id={"seq": (2 * q0 + p) * LOW + l},
+            device_id_type=mesh_id,
+        )
+
+    def weight_swap(owner, half, c):
+        ref = weights.at[owner, weight_rows(half, c)]
+        return pltpu.make_async_remote_copy(
+            src_ref=ref,
+            dst_ref=ref,
+            send_sem=swap_s.at[owner, c],
+            recv_sem=weight_r.at[owner, half, c],
+            device_id={"groups": flip(lax.axis_index("groups"))},
+            device_id_type=mesh_id,
+        )
+
+    halves = [x] if paired else [0, 1]
+    lower = [(d, c, half) for d in range(1, squares) for c in range(chunks) for half in halves]
+
+    def send_weights(up, some):
+        for d, c, half in some:
+            q0 = (q + d) % squares
+
+            @pl.when((q0 > q) if up else (q0 < q))
+            def _():
+                weight_copy(q0, half, c, q).start()
+
+    early = [one for one in lower if one[1] < (chunks + 1) // 2]
+    late = [one for one in lower if one[1] >= (chunks + 1) // 2]
+
+    for one in loads:
+        one.wait()
+    for g in range(heads):
+        @pl.when(h + 1 < high)
+        def _():
+            kv_copy(0, g, h, l).start()
+
+        @pl.when(l == 0)
+        def _():
+            kv_copy(1, g, h, l).start()
+    for d in range(seq):
+        for e0 in range(2):
+            if d > 0:
+                meta_copy(d, e0, (me, e)).start()
+    pltpu.make_async_remote_copy(
+        src_ref=meta_all.at[h, l, e],
+        dst_ref=meta_all.at[h, l, e],
+        send_sem=meta_s.at[me, 1 - e],
+        recv_sem=meta_r.at[me, e],
+        device_id={"exp": 1 - e},
+        device_id_type=mesh_id,
+    ).start()
+    weight_load.wait()
+    send_weights(False, early)
+    query_load.wait()
+
+    def half_rows(r):
+        step = span // 2
+        return pl.ds(r * step, step)
+
+    def context_copy(way, g, p0, l0, r):
+        ref = contexts.at[p0, l0, g, half_rows(r)]
+        target = ({"seq": (2 * q + 1 - p) * LOW + l}, {"seq": h * LOW + 1 - l})[way]
+        return pltpu.make_async_remote_copy(
+            src_ref=ref,
+            dst_ref=ref,
+            send_sem=ctx_s.at[way, g, p0, l0, r],
+            recv_sem=ctx_r.at[g, p0, l0, r],
+            device_id=target,
+            device_id_type=mesh_id,
+        )
+
+    for g in range(heads):
+        queries = jnp.concatenate(
             [query_ref[:, pl.ds((g * per_group + i) * HD, HD)] for i in range(per_group)], axis=0
         )
 
-        def piece(b, state, masked):
-            largest, total, summed = state
-            k = kv_ref[b // LOW, b % LOW, :, pl.ds(g * HD, HD)]
-            v = kv_ref[b // LOW, b % LOW, :, pl.ds(half + g * HD, HD)]
-            scores = lax.dot_general(
-                q, k, (((1,), (1,)), ((), ())), preferred_element_type=jnp.float32
-            ) * scale
-            if masked:
-                row = lax.broadcasted_iota(jnp.int32, scores.shape, 0) % rows
-                column = lax.broadcasted_iota(jnp.int32, scores.shape, 1)
-                scores = jnp.where(column <= row, scores, neg_large)
-            new = jnp.maximum(largest, jnp.max(scores, axis=-1, keepdims=True))
-            rescale = jnp.exp(largest - new)
-            exps = jnp.exp(scores - new)
-            total = total * rescale + jnp.sum(exps, axis=-1, keepdims=True)
-            summed = summed * rescale + jnp.dot(
-                exps.astype(jnp.bfloat16), v, preferred_element_type=jnp.float32
-            )
-            return new, total, summed
-
+        def pair_of(h0):
+            both = kv[g, h0].reshape(LOW * span, 2 * HD)
+            return both[:, :HD], both[:, HD:]
+
+        def across(h0):
+            kv_copy(1, g, h0, 1 - l).wait_recv()
+
+        stacked = per_group * span
         state = (
             jnp.full((stacked, 1), neg_large, jnp.float32),
             jnp.zeros((stacked, 1), jnp.float32),
             jnp.zeros((stacked, HD), jnp.float32),
         )
-        state = piece(me, state, True)
-        state = lax.fori_loop(0, me, lambda b, s: piece(b, s, False), state)
-        result = (state[2] / state[1]).astype(out_ref.dtype)
+
+        @pl.when(l == 1)
+        def _():
+            across(h)
+
+        k, v = pair_of(h)
+        row = lax.broadcasted_iota(jnp.int32, (stacked, LOW * span), 0) % span
+        column = lax.broadcasted_iota(jnp.int32, (stacked, LOW * span), 1)
+        state = attend_piece(queries, k, v, state, column <= row + l * span)
+
+        def step(t, state):
+            h0 = h - t
+            kv_copy(0, g, h0, l).wait_recv()
+
+            @pl.when(h + 1 < high)
+            def _():
+                kv_copy(0, g, h0, l).start()
+
+            kv_copy(1, g, h0, l).start()
+            across(h0)
+            k, v = pair_of(h0)
+            return attend_piece(queries, k, v, state, None)
+
+        state = lax.fori_loop(1, h + 1, step, state)
+        result = (state[2] / state[1]).astype(contexts.dtype)
         for i in range(per_group):
-            out_ref[:, pl.ds((g * per_group + i) * HD, HD)] = result[i * rows : (i + 1) * rows]
-        done(g)
-
-
-def front_kernel(
-    high, key_in, value_in, ids_ref, gates_ref, query_ref, weight_in, stream_ref, gain_ref,
-    mixed_ref, normed_ref, meta_all,
-    kv_all, weights, context, contexts, part, mine, ready, landed,
-    kv_r, meta_r, kv_s, meta_s, local, weight_sem, line_s, line_r, over_s, over_r, away_s, away_r
-):
-    h, l, e = split_position()
-    mesh_id = pl.DeviceIdType.MESH
-    half = key_in.shape[1]
-    top = ids_ref.shape[1]
-    copies = [
-        pltpu.make_async_copy(key_in, kv_all.at[h, l, :, pl.ds(0, half)], local.at[0]),
-        pltpu.make_async_copy(value_in, kv_all.at[h, l, :, pl.ds(half, half)], local.at[1]),
-        pltpu.make_async_copy(weight_in, weights.at[l], local.at[2]),
-    ]
-    for one in copies:
-        one.start()
-    meta_all[h, l, e] = jnp.zeros_like(meta_all[h, l, e])
-    meta_all[h, l, e, :, pl.ds(0, top)] = ids_ref[...].astype(jnp.float32)
-    meta_all[h, l, e, :, pl.ds(top, top)] = gates_ref[...]
-    all_barrier(high, h, l, e)
-    for one in copies:
-        one.wait()
-    gather_steps(
-        high, (kv_all, meta_all), (False, True), (2, 1), (kv_r, meta_r), (kv_s, meta_s), h, l, e
-    )
-    weight_copy = pltpu.make_async_remote_copy(
-        src_ref=weights.at[l],
-        dst_ref=weights.at[l],
-        send_sem=weight_sem.at[0],
-        recv_sem=weight_sem.at[1],
-        device_id={"seq": h * LOW + 1 - l},
+            contexts[p, l, g, :, pl.ds(i * HD, HD)] = result[i * span : (i + 1) * span]
+        for r in range(2):
+            context_copy(1, g, p, l, r).start()
+            context_copy(0, g, p, l, 1 - r).start()
+        if g == 0:
+            send_weights(False, late)
+    send_weights(True, lower)
+
+    for g in range(heads):
+        for r in range(2):
+            context_copy(1, g, p, 1 - l, r).wait_recv()
+            if r == 0:
+                context_copy(0, g, p, 1 - l, r).start()
+            context_copy(0, g, 1 - p, l, 1 - r).wait_recv()
+            if r == 0:
+                context_copy(1, g, 1 - p, l, 1 - r).start()
+
+    def project(d, last):
+        owner = (q + d) % squares
+        for i in range(2):
+            l0 = l if i else 1 - l
+            product = None
+            for g in range(heads):
+                term = lax.dot_general(
+                    contexts[:, l0, g].reshape(2 * span, wide),
+                    weights[owner, :, pl.ds(g * wide, wide)],
+                    (((1,), (1,)), ((), ())),
+                    preferred_element_type=jnp.float32,
+                )
+                product = term if product is None else product + term
+            product = product.astype(part.dtype)
+            for p0 in range(2):
+                for e0 in range(2):
+                    start = p0 * span + e0 * rows_e
+                    part[p0, l0, e0, owner] = product[start : start + rows_e]
+            if last:
+                for p0 in range(2):
+                    over(p0, l0).start()
+
+    def over(p0, l0):
+        return pltpu.make_async_remote_copy(
+            src_ref=part.at[p0, l0, 1 - e],
+            dst_ref=mine.at[p0, l0],
+            send_sem=over_s.at[p0, l0],
+            recv_sem=over_r.at[p0, l0],
+            device_id={"exp": 1 - e},
+            device_id_type=mesh_id,
+        )
+
+    def forward(some):
+        for d, c, half in some:
+            owner = (q + d) % squares
+            weight_copy(owner, half, c, owner).wait_recv()
+            if paired:
+                weight_swap(owner, half, c).start()
+
+    split = max(1, len(lower) * 3 // 4) if lower else 0
+    forward(lower[:split])
+    for g in range(heads):
+        context_copy(0, g, 1 - p, 1 - l, 0).wait_recv()
+        context_copy(1, g, 1 - p, 1 - l, 1).wait_recv()
+    project(0, squares == 1)
+    forward(lower[split:])
+    for d in range(1, squares):
+        for c in range(chunks):
+            if paired:
+                weight_swap((q + d) % squares, 1 - x, c).wait_recv()
+        project(d, d == squares - 1)
+
+    def away(p0, l0, p1, l1):
+        return pltpu.make_async_remote_copy(
+            src_ref=ready.at[p0, l0],
+            dst_ref=landed.at[p1, l1],
+            send_sem=away_s.at[p0, l0],
+            recv_sem=away_r.at[p1, l1],
+            device_id={"seq": (2 * q + p0) * LOW + l0},
+            device_id_type=mesh_id,
+        )
+
+    others = ((1 - p, 1 - l), (p, 1 - l), (1 - p, l))
+    for p0, l0 in others + ((p, l),):
+        over(p0, l0).wait_recv()
+    for p0, l0 in others:
+        total = part[p0, l0, e].astype(jnp.float32) + mine[p0, l0].astype(jnp.float32)
+        ready[p0, l0] = total.astype(ready.dtype)
+        away(p0, l0, p, l).start()
+    landed[p, l] = (part[p, l, e].astype(jnp.float32) + mine[p, l].astype(jnp.float32)).astype(landed.dtype)
+    stream_load.wait()
+    for p0, l0 in others:
+        away(p0, l0, p0, l0).wait_recv()
+    squared = None
+    for h0 in range(high):
+        block = pl.ds(h0 * LOW * features, LOW * features)
+        pair = jnp.concatenate([landed[h0 % 2, l0, h0 // 2] for l0 in range(LOW)], axis=1)
+        value = stream_ref[:, block].astype(jnp.float32) + pair.astype(jnp.float32)
+        mixed_ref[:, block] = value
+        term = jnp.sum(value * value, axis=-1, keepdims=True)
+        squared = term if squared is None else squared + term
+    factor = lax.rsqrt(squared / (high * LOW * features) + 1e-06)
+    for h0 in range(high):
+        block = pl.ds(h0 * LOW * features, LOW * features)
+        normed_ref[:, block] = (mixed_ref[:, block] * factor * gain_ref[:, block]).astype(
+            normed_ref.dtype
+        )
+
+    for d in range(seq):
+        for e0 in range(2):
+            if d > 0:
+                meta_copy(d, e0, ((me + d) % seq, e0)).wait_recv()
+                meta_copy(d, e0, (me, e)).wait_send()
+    peer = pltpu.make_async_remote_copy(
+        src_ref=meta_all.at[h, l, e],
+        dst_ref=meta_all.at[h, l, e],
+        send_sem=meta_s.at[me, 1 - e],
+        recv_sem=meta_r.at[me, 1 - e],
+        device_id={"exp": 1 - e},
         device_id_type=mesh_id,
     )
-    weight_copy.start()
-    parts = half // HD
-    columns = context.shape[1] // parts
-
-    def hop(way, h0, c):
-        ref = contexts.at[h0, :, pl.ds(c * columns, columns)]
-        return pltpu.make_async_remote_copy(
-            src_ref=ref,
-            dst_ref=ref,
-            send_sem=line_s.at[way, h0, c],
-            recv_sem=line_r.at[h0, c],
-            device_id={"seq": (h + 1 - 2 * way) * LOW + l},
-            device_id_type=mesh_id,
-        )
-
-    def hops(h0, c, right, left):
-        if right:
+    peer.wait_recv()
+    peer.wait_send()
+    for g in range(heads):
+        @pl.when(h + 1 < high)
+        def _():
+            kv_copy(0, g, h, l).wait_send()
+
+        @pl.when(l == 0)
+        def _():
+            kv_copy(1, g, h, l).wait_send()
+
+        @pl.loop(1, h + 1)
+        def _(t):
             @pl.when(h + 1 < high)
             def _():
-                hop(0, h0, c).start()
-        if left:
-            @pl.when(h > 0)
-            def _():
-                hop(1, h0, c).start()
-
-    def done(c):
-        at = pl.ds(c * columns, columns)
-        own = pltpu.make_async_copy(context.at[:, at], contexts.at[h, :, at], local.at[0])
-        own.start()
-        own.wait()
-        hops(h, c, True, True)
-
-    attend(query_ref, kv_all, context, h * LOW + l, done)
-    for t in range(1, high):
-        for c in range(parts):
-            @pl.when(h - t >= 0)
-            def _():
-                hop(0, h - t, c).wait_recv()
-                hops(h - t, c, True, False)
-
-            @pl.when(h + t < high)
-            def _():
-                hop(1, h + t, c).wait_recv()
-                hops(h + t, c, False, True)
-    weight_back = pltpu.make_async_remote_copy(
-        src_ref=weights.at[1 - l],
-        dst_ref=weights.at[1 - l],
-        send_sem=weight_sem.at[0],
-        recv_sem=weight_sem.at[1],
-        device_id={"seq": h * LOW + 1 - l},
-        device_id_type=mesh_id,
-    )
-    weight_back.wait_recv()
-    rows_e, features = part.shape[2:]
-    slim = features // LOW
-
-    def over(h0):
-        return pltpu.make_async_remote_copy(
-            src_ref=part.at[h0, 1 - e],
-            dst_ref=mine.at[h0],
-            send_sem=over_s.at[h0],
-            recv_sem=over_r.at[h0],
-            device_id={"exp": 1 - e},
-            device_id_type=mesh_id,
-        )
-
-    def away(h0, source):
-        return pltpu.make_async_remote_copy(
-            src_ref=ready.at[h0],
-            dst_ref=landed.at[source],
-            send_sem=away_s.at[h0],
-            recv_sem=away_r.at[source],
-            device_id={"seq": h0 * LOW + l},
-            device_id_type=mesh_id,
-        )
-
-    @pl.loop(0, high)
-    def _(d):
-        h0 = (h + 1 + d) % high
-        for l0 in range(LOW):
-            product = lax.dot_general(
-                contexts[h0], weights[l0], (((1,), (1,)), ((), ())), preferred_element_type=jnp.float32
-            ).astype(part.dtype)
-            for e0 in range(2):
-                part[h0, e0, :, pl.ds(l0 * slim, slim)] = product[e0 * rows_e : (e0 + 1) * rows_e]
-        over(h0).start()
-
-    for d in range(1, high + 1):
-        h0 = (h + d) % high
-        over(h0).wait_recv()
-        total = part[h0, e].astype(jnp.float32) + mine[h0].astype(jnp.float32)
-        ready[h0] = total.astype(ready.dtype)
-        if d < high:
-            away(h0, h).start()
-    landed[h] = ready[h]
-    for d in range(1, high):
-        away((h + d) % high, (h + high - d) % high).wait_recv()
-    squares = None
-    for h0 in range(high):
-        block = pl.ds(h0 * features, features)
-        value = stream_ref[:, block].astype(jnp.float32) + landed[h0].astype(jnp.float32)
-        mixed_ref[:, block] = value
-        term = jnp.sum(value * value, axis=-1, keepdims=True)
-        squares = term if squares is None else squares + term
-    factor = lax.rsqrt(squares / (high * features) + 1e-06)
-    for h0 in range(high):
-        block = pl.ds(h0 * features, features)
-        normed_ref[:, block] = (mixed_ref[:, block] * factor * gain_ref[:, block]).astype(
-            normed_ref.dtype
-        )
-    weight_copy.wait_send()
-    for h0 in range(high):
-        over(h0).wait_send()
-        for c in range(parts):
-            @pl.when((h + 1 < high) & (h0 <= h))
-            def _():
-                hop(0, h0, c).wait_send()
-
-            @pl.when((h > 0) & (h0 >= h))
-            def _():
-                hop(1, h0, c).wait_send()
-    for d in range(1, high):
-        away((h + d) % high, h).wait_send()
-
-
-def front(keys, values, ids, gates, queries, weight, stream, gain, high):
+                kv_copy(0, g, h - t, l).wait_send()
+
+            kv_copy(1, g, h - t, l).wait_send()
+
+        for way in range(2):
+            for r in range(2):
+                context_copy(way, g, p, l, r).wait_send()
+        context_copy(0, g, p, 1 - l, 0).wait_send()
+        context_copy(1, g, 1 - p, l, 1).wait_send()
+    for d, c, half in lower:
+        weight_copy((q + d) % squares, half, c, q).wait_send()
+        if paired:
+            weight_swap((q + d) % squares, half, c).wait_send()
+    for p0, l0 in others:
+        away(p0, l0, p, l).wait_send()
+    for p0, l0 in others + ((p, l),):
+        over(p0, l0).wait_send()
+
+
+def front(keys, values, ids, gates, queries, weight, stream, gain, high, groups):
     whole = pl.BlockSpec(memory_space=pltpu.VMEM)
-    span = queries.shape[0]
+    away = pl.BlockSpec(memory_space=pl.ANY)
+    span, columns = queries.shape
     rows = stream.shape[0]
-    features = weight.shape[0] * LOW
+    features = weight.shape[0]
+    heads = keys.shape[1] // HD
+    squares = high // 2
+    chunks = 4 if features % 128 == 0 else 1
     kind = jnp.bfloat16
     sem = pltpu.SemaphoreType.DMA
     return pl.pallas_call(
-        functools.partial(front_kernel, high),
+        functools.partial(front_kernel, high, groups, chunks),
         out_shape=(
             jax.ShapeDtypeStruct(stream.shape, jnp.float32),
             jax.ShapeDtypeStruct(stream.shape, kind),
-            jax.ShapeDtypeStruct((high, LOW, 2, rows, 128), jnp.float32),
+            jax.ShapeDtypeStruct((high, LOW, 2, 2 * ids.shape[0], 2 * rows), kind),
         ),
-        in_specs=[whole] * 8,
+        in_specs=[away, away, whole, whole, away, away, away, whole],
         out_specs=(whole,) * 3,
         scratch_shapes=[
-            pltpu.VMEM((high, LOW, span, 2 * keys.shape[1]), kind),
-            pltpu.VMEM((LOW,) + weight.shape, kind),
             pltpu.VMEM(queries.shape, kind),
-            pltpu.VMEM((high,) + queries.shape, kind),
-            pltpu.VMEM((high, 2, rows, features), kind),
-            pltpu.VMEM((high, rows, features), kind),
-            pltpu.VMEM((high, rows, features), kind),
-            pltpu.VMEM((high, rows, features), kind),
-            sem((high, LOW, 2, 2)),
-            sem((high, LOW, 2, 1)),
-            sem((4, high, LOW, 2)),
-            sem((4, high, LOW, 1)),
-            sem((3,)),
-            sem((2,)),
-            sem((2, high, keys.shape[1] // HD)),
-            sem((high, keys.shape[1] // HD)),
-            sem((high,)),
-            sem((high,)),
-            sem((high,)),
-            sem((high,)),
+            pltpu.VMEM(stream.shape, kind),
+            pltpu.VMEM((heads, high, LOW, span, 2 * HD), kind),
+            pltpu.VMEM((squares,) + weight.shape, kind),
+            pltpu.VMEM((2, LOW, heads, span, columns // heads), kind),
+            pltpu.VMEM((2, LOW, 2, squares, rows, features), kind),
+            pltpu.VMEM((2, LOW, squares, rows, features), kind),
+            pltpu.VMEM((2, LOW, squares, rows, features), kind),
+            pltpu.VMEM((2, LOW, squares, rows, features), kind),
+            sem((2 * heads + 3,)),
+            sem((high * LOW, 2)),
+            sem((high * LOW, 2)),
+            sem((2, heads, high, LOW)),
+            sem((heads, high, LOW)),
+            sem((2, heads, 2, LOW, 2)),
+            sem((heads, 2, LOW, 2)),
+            sem((squares, 2, chunks)),
+            sem((squares, 2, chunks)),
+            sem((squares, chunks)),
+            sem((2, LOW)),
+            sem((2, LOW)),
+            sem((2, LOW)),
+            sem((2, LOW)),
         ],
         compiler_params=pltpu.CompilerParams(
             collective_id=1, has_side_effects=True, vmem_limit_bytes=VMEM_LIMIT
@@ -420,34 +598,39 @@
     span = every.shape[3]
 
     def build(h0):
-        meta = meta_ref[h0].reshape(tokens_here, 128)
-        moved = pltpu.roll(meta, 128 - top, axis=1)
-        lane = lax.broadcasted_iota(jnp.int32, meta.shape, 1)
-        chosen, gates, table = [], [], jnp.zeros_like(meta)
+        meta = jnp.concatenate(
+            [
+                meta_ref[h0, l0, 0].astype(jnp.float32) + meta_ref[h0, l0, 1].astype(jnp.float32)
+                for l0 in range(LOW)
+            ],
+            axis=1,
+        )
+        ids, gates = meta[:top], meta[top:]
+        chosen, shares = [], []
         for i in range(experts):
-            here = (device * experts + i).astype(jnp.float32)
-            hit = (meta == here) & (lane < top)
-            chosen.append(jnp.sum(jnp.where(hit, 1.0, 0.0), axis=1, keepdims=True))
-            gates.append(jnp.sum(jnp.where(hit, moved, 0.0), axis=1, keepdims=True))
-            table = table + jnp.where(lane == i, chosen[i], 0.0)
+            hit = ids == (device * experts + i).astype(jnp.float32)
+            chosen.append(jnp.sum(jnp.where(hit, 1.0, 0.0), axis=0, keepdims=True))
+            shares.append(jnp.sum(jnp.where(hit, gates, 0.0), axis=0, keepdims=True))
+        line_up = jnp.concatenate(
+            chosen + [jnp.zeros_like(chosen[0])] * (-experts % 8), axis=0
+        )
         square = (tokens_here, tokens_here)
         row = lax.broadcasted_iota(jnp.int32, square, 0)
         column = lax.broadcasted_iota(jnp.int32, square, 1)
-        earlier = jnp.where((column < row) & (row // span == column // span), 1.0, 0.0)
+        earlier = jnp.where((row < column) & (row // span == column // span), 1.0, 0.0)
         place = jnp.dot(
-            earlier.astype(jnp.bfloat16), table.astype(jnp.bfloat16), preferred_element_type=jnp.float32
-        )
-        wide = (tokens_here, -(-total // 128) * 128)
-        number = lax.broadcasted_iota(jnp.int32, wide, 1).astype(jnp.float32)
-        block = (lax.broadcasted_iota(jnp.int32, (tokens_here, 1), 0) // span).astype(jnp.float32)
-        onehot, weigh = jnp.zeros(wide, jnp.float32), jnp.zeros(wide, jnp.float32)
+            line_up.astype(jnp.bfloat16), earlier.astype(jnp.bfloat16), preferred_element_type=jnp.float32
+        )
+        tall = (-(-total // 128) * 128, tokens_here)
+        number = lax.broadcasted_iota(jnp.int32, tall, 0).astype(jnp.float32)
+        block = (lax.broadcasted_iota(jnp.int32, (1, tokens_here), 1) // span).astype(jnp.float32)
+        onehot, weigh = jnp.zeros(tall, jnp.float32), jnp.zeros(tall, jnp.float32)
         for i in range(experts):
-            within = jnp.sum(jnp.where(lane == i, place, 0.0), axis=1, keepdims=True)
-            match = (number == within + block * CAP + i * slots) & (chosen[i] > 0.5)
+            match = (number == place[i : i + 1] + block * CAP + i * slots) & (chosen[i] > 0.5)
             onehot = onehot + jnp.where(match, 1.0, 0.0)
-            weigh = weigh + jnp.where(match, gates[i], 0.0)
-        combine_ref[h0] = weigh[:, :total].astype(combine_ref.dtype)
-        choose_ref[h0] = jnp.transpose(onehot)[:total].astype(choose_ref.dtype)
+            weigh = weigh + jnp.where(match, shares[i], 0.0)
+        choose_ref[h0] = onehot[:total].astype(choose_ref.dtype)
+        combine_ref[h0] = jnp.transpose(weigh)[:, :total].astype(combine_ref.dtype)
 
     gather_steps(high, (every,), (True,), (parts,), (recv,), (send,), h, l, e, build)
     for one in loads:
@@ -682,8 +865,8 @@
 ):
     high = lax.axis_size("seq") // LOW
     mixed, normed, meta = front(
-        key_rows, value_rows, expert_ids, gate_weights, queries, out_weight, stream,
-        norm_gain.reshape(1, -1), high,
+        key_rows, value_rows, expert_ids.T, gate_weights.T, queries, out_weight, stream,
+        norm_gain.reshape(1, -1), high, lax.axis_size("groups"),
     )
     return back(normed, mixed, meta, expert_in, expert_out, high, expert_ids.shape[1])
 

time: 152 us -> 139 us (0.914)
  Pallas kernels: 146 us -> 135 us
  local copies, waits for them, and re-layouts: 4.43 us -> 1.67 us
    pallas_call x1, Pallas kernels: 71.7 us -> 59.4 us  [front(): pl.pallas_call(functools.partial(front_kernel, high, groups, chunks), out...]
    unnamed x3 -> x1, local copies, waits for them, and re-layouts: 4.43 us -> 1.67 us
    pallas_call x1, Pallas kernels: 74 us -> 75.8 us  [back(): pl.pallas_call(functools.partial(back_kernel, high, parts, top), out_shap...]
where the time goes in v1:
time: 139 us; the launch traced here: 137 us
  Pallas kernels  135 us (97%)
  local copies, waits for them, and re-layouts  1.67 us (1%)
    pallas_call x1, Pallas kernels, back(): pl.pallas_call(functools.partial(back_kernel, high, parts, top), out_shap...  75.8 us
    pallas_call x1, Pallas kernels, front(): pl.pallas_call(functools.partial(front_kernel, high, groups, chunks), out...  59.4 us

profile of v1, /device:TPU:9, one launch (start us, length us, event | category | flops | bytes accessed | tf_op | source)
XLA Modules:
  0.0 136.8 jit_solution(13448759111950486775)
XLA Ops:
  0.0 59.4 %front.1 = (f32[64,2048]{1,0:T(8,128)}, bf16[64,2048]{1,0:T(8,128)(2,1)}, bf16[4,2,2,16,128]{4,3,2,1,0:T(8,128)(2,1)}) custom-call(bf16[128,256]{1,0:T(8,128)(2,1)} %key_in.1, bf16[128,256]{1,0:T(8,128)(2,1)} %value_in.1, s32[8,64]{1,0:T(8,128)} %bitcast.4, f32[8,64]{1,0:T(8,128)} %bitcast.5, bf16[128,2048]{1,0:T(8,128)(2,1)} %query_in.1, ...), custom_call_target="tpu_custom_call" | custom-call | tf_op jit(solution)/shard_map/front/pallas_call | solution.py:536
  59.4 75.8 %back.1 = bf16[64,2048]{1,0:T(8,128)(2,1)} custom-call(bf16[64,2048]{1,0:T(8,128)(2,1)} %get-tuple-element.8.normed_ref, f32[64,2048]{1,0:T(8,128)} %get-tuple-element.9.mixed_ref, bf16[4,2,2,16,128]{4,3,2,1,0:T(8,128)(2,1)} %get-tuple-element.10.meta_ref, bf16[4,2048,1536]{2,1,0:T(8,128)(2,1)} %first_hbm.1, bf16[4,768,2048]{2,1,0:T(8,128)(2,1)} %second_hbm.1), custom_call_target="tpu_custom_call" | custom-call | tf_op jit(solution)/shard_map/back/pallas_call | solution.py:821
  135.1 1.7 %copy.12 = bf16[64,2048]{1,0:T(8,128)(2,1)} copy(bf16[64,2048]{1,0:T(8,128)(2,1)} %back.1) | data formatting | bytes 524288

commit v2 on v1

--- a/solution.py
+++ b/solution.py
@@ -40,99 +40,6 @@
 
     ends = jnp.where(h + 1 < high, 1, 0) + jnp.where(h > 0, 1, 0)
     pl.semaphore_wait(barrier, ends + 2)
-
-
-def gather_steps(high, outs, cross, parts, recv, send, h, l, e, beside=None):
-    count = len(outs)
-
-    def slot(a, h0, l0, e0, c):
-        rows = outs[a].shape[-2] // parts[a]
-        at = (h0, l0, e0) if cross[a] else (h0, l0)
-        return outs[a].at[at + (pl.ds(c * rows, rows),)]
-
-    def copy(a, h0, l0, e0, c, way):
-        target = (
-            {"seq": (h + 1) * LOW + l},
-            {"seq": (h - 1) * LOW + l},
-            {"seq": h * LOW + 1 - l},
-            {"exp": 1 - e},
-        )[way]
-        ref = slot(a, h0, l0, e0, c)
-        return pltpu.make_async_remote_copy(
-            src_ref=ref,
-            dst_ref=ref,
-            send_sem=send[a].at[way, h0, l0, c],
-            recv_sem=recv[a].at[h0, l0, e0, c],
-            device_id=target,
-            device_id_type=pl.DeviceIdType.MESH,
-        )
-
-    def pass_on(a, h0, c, right, left):
-        if right:
-            @pl.when(h + 1 < high)
-            def _():
-                copy(a, h0, l, e, c, 0).start()
-        if left:
-            @pl.when(h > 0)
-            def _():
-                copy(a, h0, l, e, c, 1).start()
-        copy(a, h0, l, e, c, 2).start()
-        if cross[a]:
-            copy(a, h0, l, e, c, 3).start()
-
-    def from_across(a, h0, c):
-        copy(a, h0, 1 - l, e, c, 2).wait_recv()
-        if cross[a]:
-            copy(a, h0, 1 - l, e, c, 3).start()
-
-    for a in range(count):
-        for c in range(parts[a]):
-            pass_on(a, h, c, True, True)
-    if beside is not None:
-        beside(0)
-    for t in range(1, high + 1):
-        if t < high:
-            for a in range(count):
-                for c in range(parts[a]):
-                    @pl.when(h - t >= 0)
-                    def _():
-                        copy(a, h - t, l, e, c, 0).wait_recv()
-                        pass_on(a, h - t, c, True, False)
-
-                    @pl.when(h + t < high)
-                    def _():
-                        copy(a, h + t, l, e, c, 1).wait_recv()
-                        pass_on(a, h + t, c, False, True)
-        for a in range(count):
-            for c in range(parts[a]):
-                if t == 1:
-                    from_across(a, h, c)
-                else:
-                    @pl.when(h - t + 1 >= 0)
-                    def _():
-                        from_across(a, h - t + 1, c)
-
-                    @pl.when(h + t - 1 < high)
-                    def _():
-                        from_across(a, h + t - 1, c)
-        if beside is not None and t < high:
-            beside(t)
-    for a in range(count):
-        for c in range(parts[a]):
-            for h0 in range(high):
-                if cross[a]:
-                    for l0 in range(LOW):
-                        copy(a, h0, l0, 1 - e, c, 3).wait_recv()
-                        copy(a, h0, l0, e, c, 3).wait_send()
-                copy(a, h0, l, e, c, 2).wait_send()
-
-                @pl.when((h + 1 < high) & (h0 <= h))
-                def _():
-                    copy(a, h0, l, e, c, 0).wait_send()
-
-                @pl.when((h > 0) & (h0 >= h))
-                def _():
-                    copy(a, h0, l, e, c, 1).wait_send()
 
 
 def whole_barrier(seq, groups):
@@ -180,7 +87,7 @@
     mixed_ref, normed_ref, meta_all,
     query_ref, stream_ref, kv, weights, contexts, part, mine, ready, landed,
     local, meta_s, meta_r, kv_s, kv_r, ctx_s, ctx_r, weight_s, weight_r, swap_s, over_s, over_r,
-    away_s, away_r
+    away_s, away_r, turn
 ):
     h, l, e = split_position()
     q, p = h // 2, h % 2
@@ -214,7 +121,7 @@
     listed = jnp.concatenate([ids_ref[...].astype(jnp.float32), gates_ref[...]], axis=0)
     blank = jnp.zeros_like(listed)
     meta_all[h, l, e] = jnp.where(
-        e == 0,
+        l == 0,
         jnp.concatenate([listed, blank], axis=1),
         jnp.concatenate([blank, listed], axis=1),
     ).astype(meta_all.dtype)
@@ -273,16 +180,13 @@
     halves = [x] if paired else [0, 1]
     lower = [(d, c, half) for d in range(1, squares) for c in range(chunks) for half in halves]
 
-    def send_weights(up, some):
-        for d, c, half in some:
+    def send_weights(up):
+        for d, c, half in lower:
             q0 = (q + d) % squares
 
             @pl.when((q0 > q) if up else (q0 < q))
             def _():
                 weight_copy(q0, half, c, q).start()
-
-    early = [one for one in lower if one[1] < (chunks + 1) // 2]
-    late = [one for one in lower if one[1] >= (chunks + 1) // 2]
 
     for one in loads:
         one.wait()
@@ -307,7 +211,10 @@
         device_id_type=mesh_id,
     ).start()
     weight_load.wait()
-    send_weights(False, early)
+    @pl.when(p == 0)
+    def _():
+        send_weights(False)
+
     query_load.wait()
 
     def half_rows(r):
@@ -326,66 +233,106 @@
             device_id_type=mesh_id,
         )
 
-    for g in range(heads):
-        queries = jnp.concatenate(
+    queries = [
+        jnp.concatenate(
             [query_ref[:, pl.ds((g * per_group + i) * HD, HD)] for i in range(per_group)], axis=0
         )
-
-        def pair_of(h0):
+        for g in range(heads)
+    ]
+
+    def attend(h0, states, allowed):
+        result = []
+        for g in range(heads):
             both = kv[g, h0].reshape(LOW * span, 2 * HD)
-            return both[:, :HD], both[:, HD:]
-
-        def across(h0):
+            result.append(attend_piece(queries[g], both[:, :HD], both[:, HD:], states[g], allowed))
+        return tuple(result)
+
+    def across(h0):
+        for g in range(heads):
             kv_copy(1, g, h0, 1 - l).wait_recv()
 
-        stacked = per_group * span
-        state = (
+    def relay(h0):
+        for g in range(heads):
+            kv_copy(0, g, h0, l).wait_recv()
+
+            @pl.when(h + 1 < high)
+            def _():
+                kv_copy(0, g, h0, l).start()
+
+            kv_copy(1, g, h0, l).start()
+
+    @pl.when(h > 0)
+    def _():
+        relay(h - 1)
+
+    @pl.when(l == 1)
+    def _():
+        across(h)
+
+    stacked = per_group * span
+    states = tuple(
+        (
             jnp.full((stacked, 1), neg_large, jnp.float32),
             jnp.zeros((stacked, 1), jnp.float32),
             jnp.zeros((stacked, HD), jnp.float32),
         )
-
-        @pl.when(l == 1)
-        def _():
-            across(h)
-
-        k, v = pair_of(h)
-        row = lax.broadcasted_iota(jnp.int32, (stacked, LOW * span), 0) % span
-        column = lax.broadcasted_iota(jnp.int32, (stacked, LOW * span), 1)
-        state = attend_piece(queries, k, v, state, column <= row + l * span)
-
-        def step(t, state):
-            h0 = h - t
-            kv_copy(0, g, h0, l).wait_recv()
-
-            @pl.when(h + 1 < high)
-            def _():
-                kv_copy(0, g, h0, l).start()
-
-            kv_copy(1, g, h0, l).start()
-            across(h0)
-            k, v = pair_of(h0)
-            return attend_piece(queries, k, v, state, None)
-
-        state = lax.fori_loop(1, h + 1, step, state)
-        result = (state[2] / state[1]).astype(contexts.dtype)
+        for _ in range(heads)
+    )
+    row = lax.broadcasted_iota(jnp.int32, (stacked, LOW * span), 0) % span
+    column = lax.broadcasted_iota(jnp.int32, (stacked, LOW * span), 1)
+    states = attend(h, states, column <= row + l * span)
+
+    def step(t, states):
+        @pl.when(t < h)
+        def _():
+            relay(h - t - 1)
+
+        @pl.when((t == 1) & (p == 1))
+        def _():
+            send_weights(False)
+
+        across(h - t)
+        return attend(h - t, states, None)
+
+    states = lax.fori_loop(1, h + 1, step, states)
+    for g in range(heads):
+        @pl.when(l == 0)
+        def _():
+            kv_copy(1, g, h, l).wait_send()
+
+        @pl.loop(1, h + 1)
+        def _(t):
+            kv_copy(1, g, h - t, l).wait_send()
+
+    pl.semaphore_signal(turn, inc=1, device_id={"exp": 1 - e}, device_id_type=mesh_id)
+    pl.semaphore_wait(turn, 1)
+    for g in range(heads):
+        result = (states[g][2] / states[g][1]).astype(contexts.dtype)
         for i in range(per_group):
             contexts[p, l, g, :, pl.ds(i * HD, HD)] = result[i * span : (i + 1) * span]
         for r in range(2):
             context_copy(1, g, p, l, r).start()
             context_copy(0, g, p, l, 1 - r).start()
-        if g == 0:
-            send_weights(False, late)
-    send_weights(True, lower)
-
-    for g in range(heads):
+
+    send_weights(True)
+
+    def pass_contexts(g):
         for r in range(2):
             context_copy(1, g, p, 1 - l, r).wait_recv()
-            if r == 0:
+            if r == 0 and g == 0:
                 context_copy(0, g, p, 1 - l, r).start()
+            elif r == 0:
+                @pl.when(p == 1)
+                def _():
+                    context_copy(0, g, p, 1 - l, r).start()
+
             context_copy(0, g, 1 - p, l, 1 - r).wait_recv()
             if r == 0:
                 context_copy(1, g, 1 - p, l, 1 - r).start()
+            elif g > 0:
+                @pl.when(p == 1)
+                def _():
+                    context_copy(1, g, 1 - p, l, 1 - r).start()
 
     def project(d, last):
         owner = (q + d) % squares
@@ -426,13 +373,14 @@
             if paired:
                 weight_swap(owner, half, c).start()
 
-    split = max(1, len(lower) * 3 // 4) if lower else 0
-    forward(lower[:split])
+    split = len(lower) // 2
+    for g in range(heads):
+        pass_contexts(g)
+        forward(lower[:split] if g == 0 else lower[split:])
     for g in range(heads):
         context_copy(0, g, 1 - p, 1 - l, 0).wait_recv()
         context_copy(1, g, 1 - p, 1 - l, 1).wait_recv()
     project(0, squares == 1)
-    forward(lower[split:])
     for d in range(1, squares):
         for c in range(chunks):
             if paired:
@@ -495,22 +443,23 @@
         def _():
             kv_copy(0, g, h, l).wait_send()
 
-        @pl.when(l == 0)
-        def _():
-            kv_copy(1, g, h, l).wait_send()
-
         @pl.loop(1, h + 1)
         def _(t):
             @pl.when(h + 1 < high)
             def _():
                 kv_copy(0, g, h - t, l).wait_send()
 
-            kv_copy(1, g, h - t, l).wait_send()
-
         for way in range(2):
             for r in range(2):
                 context_copy(way, g, p, l, r).wait_send()
-        context_copy(0, g, p, 1 - l, 0).wait_send()
+        if g == 0:
+            context_copy(0, g, p, 1 - l, 0).wait_send()
+        else:
+            @pl.when(p == 1)
+            def _():
+                context_copy(0, g, p, 1 - l, 0).wait_send()
+                context_copy(1, g, 1 - p, l, 0).wait_send()
+
         context_copy(1, g, 1 - p, l, 1).wait_send()
     for d, c, half in lower:
         weight_copy((q + d) % squares, half, c, q).wait_send()
@@ -566,6 +515,7 @@
             sem((2, LOW)),
             sem((2, LOW)),
             sem((2, LOW)),
+            pltpu.SemaphoreType.REGULAR,
         ],
         compiler_params=pltpu.CompilerParams(
             collective_id=1, has_side_effects=True, vmem_limit_bytes=VMEM_LIMIT
@@ -580,28 +530,31 @@
     local, weight_sem, recv, send, near_s, near_r, across_s, across_r, line_s, line_r
 ):
     h, l, e = split_position()
+    mesh_id = pl.DeviceIdType.MESH
     experts, width, double = first.shape
     hidden = double // 2
     slots = picked.shape[2]
+    pairs = high // 2
+    span = every.shape[3]
+    rows = span // parts
     loads = []
     for i in range(experts):
         loads.append(pltpu.make_async_copy(first_hbm.at[i], first.at[i], weight_sem.at[0, i]))
         loads.append(pltpu.make_async_copy(second_hbm.at[i], second.at[i], weight_sem.at[1, i]))
     for one in loads:
         one.start()
-    own = pltpu.make_async_copy(normed_ref, every.at[h, l, e], local.at[0])
+    own = pltpu.make_async_copy(normed_ref, every.at[e, h, l], local.at[0])
     own.start()
     line_barrier(high, h, l, e)
     own.wait()
     device = (h * LOW + l) * 2 + e
-    tokens_here, total = combine_ref.shape[1:]
-    span = every.shape[3]
-
-    def build(h0):
+    tokens_here, total = combine_ref.shape[2:]
+
+    def build(a, hp):
         meta = jnp.concatenate(
             [
-                meta_ref[h0, l0, 0].astype(jnp.float32) + meta_ref[h0, l0, 1].astype(jnp.float32)
-                for l0 in range(LOW)
+                meta_ref[2 * hp + k, 0, a].astype(jnp.float32) + meta_ref[2 * hp + k, 1, a].astype(jnp.float32)
+                for k in range(2)
             ],
             axis=1,
         )
@@ -629,62 +582,156 @@
             match = (number == place[i : i + 1] + block * CAP + i * slots) & (chosen[i] > 0.5)
             onehot = onehot + jnp.where(match, 1.0, 0.0)
             weigh = weigh + jnp.where(match, shares[i], 0.0)
-        choose_ref[h0] = onehot[:total].astype(choose_ref.dtype)
-        combine_ref[h0] = jnp.transpose(weigh)[:, :total].astype(combine_ref.dtype)
-
-    gather_steps(high, (every,), (True,), (parts,), (recv,), (send,), h, l, e, build)
-    for one in loads:
-        one.wait()
-    rows_all = every.shape[1] * every.shape[2] * every.shape[3]
+        choose_ref[a, hp] = onehot[:total].astype(choose_ref.dtype)
+        combine_ref[a, hp] = jnp.transpose(weigh)[:, :total].astype(combine_ref.dtype)
+
+    def copy(h0, l0, e0, c, way):
+        target = (
+            {"seq": (h + 1) * LOW + l},
+            {"seq": (h - 1) * LOW + l},
+            {"seq": h * LOW + 1 - l},
+            {"exp": 1 - e},
+        )[way]
+        ref = every.at[e0, h0, l0, pl.ds(c * rows, rows)]
+        return pltpu.make_async_remote_copy(
+            src_ref=ref,
+            dst_ref=ref,
+            send_sem=send.at[way, h0, l0, c],
+            recv_sem=recv.at[h0, l0, e0, c],
+            device_id=target,
+            device_id_type=mesh_id,
+        )
+
+    def onward(h0, c, way):
+        @pl.when((h + 1 < high) if way == 0 else (h > 0))
+        def _():
+            copy(h0, l, e, c, way).start()
+
+    def stage(t):
+        for c in range(parts):
+            for way, h0, fits in ((0, h - t, h - t >= 0), (1, h + t, h + t < high)):
+                @pl.when(fits)
+                def _():
+                    copy(h0, l, e, c, way).wait_recv()
+                    onward(h0, c, way)
+                    copy(h0, l, e, c, 2).start()
+                    copy(h0, l, e, c, 3).start()
+
+    def from_across(t):
+        for c in range(parts):
+            for h0, fits in ((h - t, h - t >= 0), (h + t, h + t < high))[: 2 if t else 1]:
+                @pl.when(fits)
+                def _():
+                    copy(h0, 1 - l, e, c, 2).wait_recv()
+                    copy(h0, 1 - l, e, c, 3).start()
+
+    def from_core(t, l0):
+        for c in range(parts):
+            for h0, fits in ((h - t, h - t >= 0), (h + t, h + t < high))[: 2 if t else 1]:
+                @pl.when(fits)
+                def _():
+                    copy(h0, l0, 1 - e, c, 3).wait_recv()
+
+    def sent():
+        for c in range(parts):
+            for h0 in range(high):
+                for l0 in range(LOW):
+                    copy(h0, l0, e, c, 3).wait_send()
+                copy(h0, l, e, c, 2).wait_send()
+
+                @pl.when((h + 1 < high) & (h0 <= h))
+                def _():
+                    copy(h0, l, e, c, 0).wait_send()
+
+                @pl.when((h > 0) & (h0 >= h))
+                def _():
+                    copy(h0, l, e, c, 1).wait_send()
+
+    @pl.when(e == 0)
+    def _():
+        for c in range(parts):
+            onward(h, c, 0)
+            onward(h, c, 1)
+            copy(h, l, e, c, 2).start()
+            copy(h, l, e, c, 3).start()
+
+    for hp in range(pairs):
+        build(0, hp)
+
+    @pl.when(e == 0)
+    def _():
+        for t in range(1, high):
+            stage(t)
+            from_across(t - 1)
+        from_across(high - 1)
+
+    @pl.when(e == 1)
+    def _():
+        for t in range(high):
+            from_core(t, l)
+            for c in range(parts):
+                @pl.when(h == t)
+                def _():
+                    onward(h, c, 0)
+
+                @pl.when(h + t == high - 1)
+                def _():
+                    onward(h, c, 1)
+        for c in range(parts):
+            copy(h, l, e, c, 2).start()
+            copy(h, l, e, c, 3).start()
+        for t in range(high):
+            from_core(t, 1 - l)
+
     tile = 512
 
-    @pl.loop(0, high)
-    def _(h0):
-        for n in range(0, width, tile):
-            tokens = every[h0, :, :, :, pl.ds(n, tile)].reshape(rows_all, tile)
-            value = jnp.dot(choose_ref[h0], tokens, preferred_element_type=jnp.float32)
-            for i in range(experts):
-                picked[i, h0, :, pl.ds(n, tile)] = value[i * slots : (i + 1) * slots].astype(
-                    picked.dtype
+    def pick(a):
+        @pl.loop(0, pairs)
+        def _(hp):
+            for n in range(0, width, tile):
+                tokens = every[a, pl.ds(2 * hp, 2), :, :, pl.ds(n, tile)].reshape(tokens_here, tile)
+                value = jnp.dot(choose_ref[a, hp], tokens, preferred_element_type=jnp.float32)
+                for i in range(experts):
+                    picked[i, hp, :, pl.ds(n, tile)] = value[i * slots : (i + 1) * slots].astype(
+                        picked.dtype
+                    )
+
+    def run_experts(hooks):
+        def run(i, carry):
+            step = 256
+            taken = picked[i].reshape(pairs * slots, width)
+            for f in range(0, hidden, step):
+                gate = jnp.dot(taken, first[i, :, pl.ds(f, step)], preferred_element_type=jnp.float32)
+                up = jnp.dot(
+                    taken, first[i, :, pl.ds(hidden + f, step)], preferred_element_type=jnp.float32
                 )
-
-    def run(i, carry):
-        step = 256
-        rows = picked[i].reshape(high * slots, width)
-        for f in range(0, hidden, step):
-            gate = jnp.dot(rows, first[i, :, pl.ds(f, step)], preferred_element_type=jnp.float32)
-            up = jnp.dot(
-                rows, first[i, :, pl.ds(hidden + f, step)], preferred_element_type=jnp.float32
-            )
-            act[:, pl.ds(f, step)] = (gate / (1.0 + jnp.exp(-gate)) * up).astype(act.dtype)
-        for n in range(0, width, tile):
-            value = jnp.dot(
-                act[...], second[i, :, pl.ds(n, tile)], preferred_element_type=jnp.float32
-            ).astype(picked.dtype)
-            picked[i, :, :, pl.ds(n, tile)] = value.reshape(high, slots, tile)
-        return carry
-
-    lax.fori_loop(0, experts, run, 0)
-    scatter_steps(
-        high, parts, every, mixed_ref, out_ref, near, sums, across, running, line,
-        near_s, near_r, across_s, across_r, line_s, line_r, h, l, e, combine_ref, picked, tile
-    )
-
-
-def scatter_steps(
-    high, parts, part_ref, mixed_ref, out_ref, near, sums, across, running, line,
-    near_s, near_r, across_s, across_r, line_s, line_r, h, l, e, combine_ref, picked, tile
-):
-    rows = part_ref.shape[-2] // parts
-    mesh_id = pl.DeviceIdType.MESH
+                act[:, pl.ds(f, step)] = (gate / (1.0 + jnp.exp(-gate)) * up).astype(act.dtype)
+            for n in range(0, width, tile):
+                value = jnp.dot(
+                    act[...], second[i, :, pl.ds(n, tile)], preferred_element_type=jnp.float32
+                ).astype(picked.dtype)
+                picked[i, :, :, pl.ds(n, tile)] = value.reshape(pairs, slots, tile)
+            for k, hook in hooks:
+                @pl.when((e == 1) & (i == min(k, experts - 1)))
+                def _():
+                    hook()
+            return carry
+
+        lax.fori_loop(0, experts, run, 0)
+
     order = []
     for i in range(high):
         order.append(i // 2 if i % 2 == 0 else high - 1 - i // 2)
+    turns = []
+    for h0 in order:
+        if h0 // 2 not in turns:
+            turns.append(h0 // 2)
+    shape = (2,) + every.shape[2:4]
 
     def to_near(h0, l0, c):
         at = pl.ds(c * rows, rows)
         return pltpu.make_async_remote_copy(
-            src_ref=part_ref.at[h0, l0, 1 - e, at],
+            src_ref=every.at[1 - e, h0, l0, at],
             dst_ref=near.at[h0, l0, at],
             send_sem=near_s.at[h0, l0, c],
             recv_sem=near_r.at[h0, l0, c],
@@ -715,66 +762,123 @@
         )
 
     pieces = [(h0, c) for h0 in order for c in range(parts)]
-    experts, width = picked.shape[0], picked.shape[-1]
-    shape = part_ref.shape[1:4]
-    for h0 in order:
-        for n in range(0, width, tile):
-            rows_here = jnp.concatenate(
-                [picked[i, h0, :, pl.ds(n, tile)] for i in range(experts)], axis=0
-            )
-            value = jnp.dot(combine_ref[h0], rows_here, preferred_element_type=jnp.float32)
-            part_ref[h0, :, :, :, pl.ds(n, tile)] = value.astype(part_ref.dtype).reshape(
-                shape + (tile,)
-            )
-        for c in range(parts):
-            to_near(h0, 1 - l, c).start()
-        for c in range(parts):
-            to_near(h0, l, c).start()
-    for h0, c in pieces:
-        at = pl.ds(c * rows, rows)
-        to_near(h0, 1 - l, c).wait_recv()
-        value = part_ref[h0, 1 - l, e, at].astype(jnp.float32) + near[h0, 1 - l, at].astype(jnp.float32)
-        sums[h0, at] = value.astype(sums.dtype)
-        to_across(h0, c).start()
-    for h0, c in pieces:
-        at = pl.ds(c * rows, rows)
-        to_near(h0, l, c).wait_recv()
-        to_across(h0, c).wait_recv()
-
-        def held():
-            value = part_ref[h0, l, e, at].astype(jnp.float32) + near[h0, l, at].astype(jnp.float32)
-            return value + across[h0, at].astype(jnp.float32)
-
-        @pl.when(h0 < h)
-        def _():
-            @pl.when(h + 1 < high)
+
+    def combine(a):
+        for hp in turns:
+            for n in range(0, width, tile):
+                rows_here = jnp.concatenate(
+                    [picked[i, hp, :, pl.ds(n, tile)] for i in range(experts)], axis=0
+                )
+                value = jnp.dot(combine_ref[a, hp], rows_here, preferred_element_type=jnp.float32)
+                every[a, 2 * hp : 2 * hp + 2, :, :, pl.ds(n, tile)] = value.astype(every.dtype).reshape(
+                    shape + (tile,)
+                )
+
+            @pl.when(e != a)
             def _():
-                to_line(0, h0, c).wait_recv()
-                running[h0, at] = (held() + line[0, h0, at].astype(jnp.float32)).astype(running.dtype)
-
-            @pl.when(h + 1 >= high)
+                for l0 in (1 - l, l):
+                    for h0 in (2 * hp, 2 * hp + 1):
+                        for c in range(parts):
+                            to_near(h0, l0, c).start()
+
+    def over_y():
+        for h0, c in pieces:
+            at = pl.ds(c * rows, rows)
+            to_near(h0, 1 - l, c).wait_recv()
+            value = every[e, h0, 1 - l, at].astype(jnp.float32) + near[h0, 1 - l, at].astype(jnp.float32)
+            sums[h0, at] = value.astype(sums.dtype)
+            to_across(h0, c).start()
+
+    def along_line():
+        for h0, c in pieces:
+            at = pl.ds(c * rows, rows)
+            to_near(h0, l, c).wait_recv()
+            to_across(h0, c).wait_recv()
+
+            def held():
+                value = every[e, h0, l, at].astype(jnp.float32) + near[h0, l, at].astype(jnp.float32)
+                return value + across[h0, at].astype(jnp.float32)
+
+            @pl.when(h0 < h)
             def _():
-                running[h0, at] = held().astype(running.dtype)
-
-            to_line(0, h0, c).start()
-
-        @pl.when(h0 > h)
-        def _():
-            @pl.when(h > 0)
+                @pl.when(h + 1 < high)
+                def _():
+                    to_line(0, h0, c).wait_recv()
+                    running[h0, at] = (held() + line[0, h0, at].astype(jnp.float32)).astype(running.dtype)
+
+                @pl.when(h + 1 >= high)
+                def _():
+                    running[h0, at] = held().astype(running.dtype)
+
+                to_line(0, h0, c).start()
+
+            @pl.when(h0 > h)
             def _():
-                to_line(1, h0, c).wait_recv()
-                running[h0, at] = (held() + line[1, h0, at].astype(jnp.float32)).astype(running.dtype)
-
-            @pl.when(h <= 0)
-            def _():
-                running[h0, at] = held().astype(running.dtype)
-
-            to_line(1, h0, c).start()
+                @pl.when(h > 0)
+                def _():
+                    to_line(1, h0, c).wait_recv()
+                    running[h0, at] = (held() + line[1, h0, at].astype(jnp.float32)).astype(running.dtype)
+
+                @pl.when(h <= 0)
+                def _():
+                    running[h0, at] = held().astype(running.dtype)
+
+                to_line(1, h0, c).start()
+
+    pick(0)
+    for one in loads:
+        one.wait()
+    last = [(max(0, experts - 2), functools.partial(stage, t)) for t in range(3, high)]
+    run_experts(
+        [(0, functools.partial(stage, 1)), (0, functools.partial(from_across, 0))]
+        + [(1, functools.partial(stage, 2))] * (high > 2)
+        + last
+        + [(2, functools.partial(from_across, 1))] * (high > 1)
+    )
+
+    @pl.when(e == 0)
+    def _():
+        sent()
+
+    @pl.when(e == 1)
+    def _():
+        for t in range(2, high - 1):
+            from_across(t)
+
+    combine(0)
+    for hp in range(pairs):
+        build(1, hp)
+
+    @pl.when(e == 1)
+    def _():
+        for t in range(max(2, high - 1), high):
+            from_across(t)
+
+    @pl.when(e == 0)
+    def _():
+        over_y()
+        for l0 in (l, 1 - l):
+            for t in range(high):
+                from_core(t, l0)
+
+    pick(1)
+    run_experts([])
+
+    @pl.when(e == 1)
+    def _():
+        sent()
+
+    combine(1)
+
+    @pl.when(e == 1)
+    def _():
+        over_y()
+
+    along_line()
     for c in range(parts):
         at = pl.ds(c * rows, rows)
-        value = part_ref[h, l, e, at].astype(jnp.float32) + near[h, l, at].astype(jnp.float32)
-        value = value + across[h, at].astype(jnp.float32) + mixed_ref[at, :]
-        mixed_ref_sum = value
+        value = every[e, h, l, at].astype(jnp.float32) + near[h, l, at].astype(jnp.float32)
+        partial = value + across[h, at].astype(jnp.float32) + mixed_ref[at, :]
 
         @pl.when(h + 1 < high)
         def _():
@@ -792,11 +896,12 @@
         def _():
             line[1, h, at] = jnp.zeros_like(line[1, h, at])
 
-        value = mixed_ref_sum + line[0, h, at].astype(jnp.float32) + line[1, h, at].astype(jnp.float32)
+        value = partial + line[0, h, at].astype(jnp.float32) + line[1, h, at].astype(jnp.float32)
         out_ref[at, :] = value.astype(out_ref.dtype)
+
     for h0, c in pieces:
-        to_near(h0, l, c).wait_send()
-        to_near(h0, 1 - l, c).wait_send()
+        for l0 in range(LOW):
+            to_near(h0, l0, c).wait_send()
         to_across(h0, c).wait_send()
 
         @pl.when(h0 < h)
@@ -818,19 +923,20 @@
     experts = expert_in.shape[0]
     slots = LOW * 2 * CAP
     tokens = LOW * 2 * rows
+    pairs = high // 2
     return pl.pallas_call(
         functools.partial(back_kernel, high, parts, top),
         out_shape=jax.ShapeDtypeStruct((rows, width), kind),
         in_specs=[whole] * 3 + [away] * 2,
         out_specs=whole,
         scratch_shapes=[
-            pltpu.VMEM((high, experts * slots, tokens), kind),
-            pltpu.VMEM((high, tokens, experts * slots), kind),
-            pltpu.VMEM((high, LOW, 2, rows, width), kind),
+            pltpu.VMEM((2, pairs, experts * slots, tokens), kind),
+            pltpu.VMEM((2, pairs, tokens, experts * slots), kind),
+            pltpu.VMEM((2, high, LOW, rows, width), kind),
             pltpu.VMEM(expert_in.shape, kind),
             pltpu.VMEM(expert_out.shape, kind),
-            pltpu.VMEM((experts, high, slots, width), kind),
-            pltpu.VMEM((high * slots, expert_out.shape[1]), kind),
+            pltpu.VMEM((experts, pairs, slots, width), kind),
+            pltpu.VMEM((pairs * slots, expert_out.shape[1]), kind),
             pltpu.VMEM((high, LOW, rows, width), kind),
             pltpu.VMEM((high, rows, width), kind),
             pltpu.VMEM((high, rows, width), kind),

time: 139 us -> 131 us (0.942); the launches traced: 137 us -> 131 us
  Pallas kernels: 135 us -> 130 us
    pallas_call x1, Pallas kernels: 59.4 us -> 50.7 us  [front(): pl.pallas_call(functools.partial(front_kernel, high, groups, chunks), out...]
    pallas_call x1, Pallas kernels: 75.8 us -> 78.8 us  [back(): pl.pallas_call(functools.partial(back_kernel, high, parts, top), out_shap...]
where the time goes in v2:
time: 131 us
  Pallas kernels  130 us (99%)
  local copies, waits for them, and re-layouts  1.67 us (1%)
    pallas_call x1, Pallas kernels, back(): pl.pallas_call(functools.partial(back_kernel, high, parts, top), out_shap...  78.8 us
    pallas_call x1, Pallas kernels, front(): pl.pallas_call(functools.partial(front_kernel, high, groups, chunks), out...  50.7 us

profile of v2, /device:TPU:9, one launch (start us, length us, event | category | flops | bytes accessed | tf_op | source)
XLA Modules:
  0.0 131.2 jit_solution(8876157151940903672)
XLA Ops:
  0.0 50.7 %front.1 = (f32[64,2048]{1,0:T(8,128)}, bf16[64,2048]{1,0:T(8,128)(2,1)}, bf16[4,2,2,16,128]{4,3,2,1,0:T(8,128)(2,1)}) custom-call(bf16[128,256]{1,0:T(8,128)(2,1)} %key_in.1, bf16[128,256]{1,0:T(8,128)(2,1)} %value_in.1, s32[8,64]{1,0:T(8,128)} %bitcast.4, f32[8,64]{1,0:T(8,128)} %bitcast.5, bf16[128,2048]{1,0:T(8,128)(2,1)} %query_in.1, ...), custom_call_target="tpu_custom_call" | custom-call | tf_op jit(solution)/shard_map/front/pallas_call | solution.py:485
  50.7 78.8 %back.1 = bf16[64,2048]{1,0:T(8,128)(2,1)} custom-call(bf16[64,2048]{1,0:T(8,128)(2,1)} %get-tuple-element.8.normed_ref, f32[64,2048]{1,0:T(8,128)} %get-tuple-element.9.mixed_ref, bf16[4,2,2,16,128]{4,3,2,1,0:T(8,128)(2,1)} %get-tuple-element.10.meta_ref, bf16[4,2048,1536]{2,1,0:T(8,128)(2,1)} %first_hbm.1, bf16[4,768,2048]{2,1,0:T(8,128)(2,1)} %second_hbm.1), custom_call_target="tpu_custom_call" | custom-call | tf_op jit(solution)/shard_map/back/pallas_call | solution.py:927
  129.5 1.7 %copy.12 = bf16[64,2048]{1,0:T(8,128)(2,1)} copy(bf16[64,2048]{1,0:T(8,128)(2,1)} %back.1) | data formatting | bytes 524288

commit v3 on v2

--- a/solution.py
+++ b/solution.py
@@ -525,9 +525,10 @@
 
 
 def back_kernel(
-    high, parts, top, normed_ref, mixed_ref, meta_ref, first_hbm, second_hbm, out_ref,
+    high, top, normed_ref, mixed_ref, meta_ref, first_hbm, second_hbm, out_ref,
     choose_ref, combine_ref, every, first, second, picked, act, near, sums, across, running, line,
-    local, weight_sem, recv, send, near_s, near_r, across_s, across_r, line_s, line_r
+    ours, given, local, weight_sem, recv, send, near_s, near_r, across_s, across_r, line_s, line_r,
+    last_s, last_r
 ):
     h, l, e = split_position()
     mesh_id = pl.DeviceIdType.MESH
@@ -535,18 +536,22 @@
     hidden = double // 2
     slots = picked.shape[2]
     pairs = high // 2
-    span = every.shape[3]
-    rows = span // parts
+    parts, rows = every.shape[3:5]
+    half = parts // 2
+    span = parts * rows
     loads = []
     for i in range(experts):
         loads.append(pltpu.make_async_copy(first_hbm.at[i], first.at[i], weight_sem.at[0, i]))
         loads.append(pltpu.make_async_copy(second_hbm.at[i], second.at[i], weight_sem.at[1, i]))
-    for one in loads:
+    owns = [
+        pltpu.make_async_copy(normed_ref.at[pl.ds(c * rows, rows)], every.at[e, h, l, c], local.at[c])
+        for c in range(parts)
+    ]
+    for one in owns + loads:
         one.start()
-    own = pltpu.make_async_copy(normed_ref, every.at[e, h, l], local.at[0])
-    own.start()
     line_barrier(high, h, l, e)
-    own.wait()
+    for one in owns:
+        one.wait()
     device = (h * LOW + l) * 2 + e
     tokens_here, total = combine_ref.shape[2:]
 
@@ -585,111 +590,133 @@
         choose_ref[a, hp] = onehot[:total].astype(choose_ref.dtype)
         combine_ref[a, hp] = jnp.transpose(weigh)[:, :total].astype(combine_ref.dtype)
 
-    def copy(h0, l0, e0, c, way):
+    mine = [e * half + j for j in range(half)]
+    theirs = [(1 - e) * half + j for j in range(half)]
+
+    def copy(a, h0, l0, c, way):
         target = (
             {"seq": (h + 1) * LOW + l},
             {"seq": (h - 1) * LOW + l},
             {"seq": h * LOW + 1 - l},
             {"exp": 1 - e},
         )[way]
-        ref = every.at[e0, h0, l0, pl.ds(c * rows, rows)]
+        ref = every.at[a, h0, l0, c]
         return pltpu.make_async_remote_copy(
             src_ref=ref,
             dst_ref=ref,
-            send_sem=send.at[way, h0, l0, c],
-            recv_sem=recv.at[h0, l0, e0, c],
+            send_sem=send.at[way, a, h0, l0, c],
+            recv_sem=recv.at[a, h0, l0, c],
             device_id=target,
             device_id_type=mesh_id,
         )
 
-    def onward(h0, c, way):
+    def onward(a, h0, c, way):
         @pl.when((h + 1 < high) if way == 0 else (h > 0))
         def _():
-            copy(h0, l, e, c, way).start()
-
-    def stage(t):
-        for c in range(parts):
-            for way, h0, fits in ((0, h - t, h - t >= 0), (1, h + t, h + t < high)):
+            copy(a, h0, l, c, way).start()
+
+    def own_z(a, way):
+        for c in mine:
+            onward(a, h, c, way)
+
+    def at_distance(t):
+        return ((0, h - t, h - t >= 0), (1, h + t, h + t < high))[: 2 if t else 1]
+
+    def stage(a, t, z=True, y=True):
+        for c in mine:
+            for way, h0, fits in at_distance(t):
                 @pl.when(fits)
                 def _():
-                    copy(h0, l, e, c, way).wait_recv()
-                    onward(h0, c, way)
-                    copy(h0, l, e, c, 2).start()
-                    copy(h0, l, e, c, 3).start()
-
-    def from_across(t):
-        for c in range(parts):
-            for h0, fits in ((h - t, h - t >= 0), (h + t, h + t < high))[: 2 if t else 1]:
+                    if z and t:
+                        copy(a, h0, l, c, way).wait_recv()
+                        onward(a, h0, c, way)
+                    if y:
+                        copy(a, h0, l, c, 2).start()
+                        if t:
+                            copy(a, h0, l, c, 3).start()
+
+    def from_across(a, t):
+        for c in mine:
+            for _, h0, fits in at_distance(t):
                 @pl.when(fits)
                 def _():
-                    copy(h0, 1 - l, e, c, 2).wait_recv()
-                    copy(h0, 1 - l, e, c, 3).start()
-
-    def from_core(t, l0):
-        for c in range(parts):
-            for h0, fits in ((h - t, h - t >= 0), (h + t, h + t < high))[: 2 if t else 1]:
-                @pl.when(fits)
-                def _():
-                    copy(h0, l0, 1 - e, c, 3).wait_recv()
-
-    def sent():
-        for c in range(parts):
+                    copy(a, h0, 1 - l, c, 2).wait_recv()
+                    copy(a, h0, 1 - l, c, 3).start()
+
+    def swapped(a):
+        @pl.when(e != a)
+        def _():
+            for c in mine:
+                copy(a, h, l, c, 3).wait_recv()
+
+    def from_core(a):
+        for c in theirs:
             for h0 in range(high):
-                for l0 in range(LOW):
-                    copy(h0, l0, e, c, 3).wait_send()
-                copy(h0, l, e, c, 2).wait_send()
+                @pl.when((h0 != h) | (e != a))
+                def _():
+                    copy(a, h0, l, c, 3).wait_recv()
+
+                copy(a, h0, 1 - l, c, 3).wait_recv()
+
+    def sent(a):
+        @pl.when(e == a)
+        def _():
+            for c in theirs:
+                copy(a, h, l, c, 3).wait_send()
+
+        for c in mine:
+            for h0 in range(high):
+                @pl.when((h0 != h) | (e == a))
+                def _():
+                    copy(a, h0, l, c, 3).wait_send()
+
+                copy(a, h0, 1 - l, c, 3).wait_send()
+                copy(a, h0, l, c, 2).wait_send()
 
                 @pl.when((h + 1 < high) & (h0 <= h))
                 def _():
-                    copy(h0, l, e, c, 0).wait_send()
+                    copy(a, h0, l, c, 0).wait_send()
 
                 @pl.when((h > 0) & (h0 >= h))
                 def _():
-                    copy(h0, l, e, c, 1).wait_send()
-
-    @pl.when(e == 0)
-    def _():
-        for c in range(parts):
-            onward(h, c, 0)
-            onward(h, c, 1)
-            copy(h, l, e, c, 2).start()
-            copy(h, l, e, c, 3).start()
-
+                    copy(a, h0, l, c, 1).wait_send()
+
+    for c in theirs + mine:
+        copy(e, h, l, c, 3).start()
+    swapped(0)
+    own_z(0, 0)
+    own_z(0, 1)
+    stage(0, 0)
     for hp in range(pairs):
         build(0, hp)
-
-    @pl.when(e == 0)
-    def _():
-        for t in range(1, high):
-            stage(t)
-            from_across(t - 1)
-        from_across(high - 1)
-
-    @pl.when(e == 1)
-    def _():
-        for t in range(high):
-            from_core(t, l)
-            for c in range(parts):
-                @pl.when(h == t)
-                def _():
-                    onward(h, c, 0)
-
-                @pl.when(h + t == high - 1)
-                def _():
-                    onward(h, c, 1)
-        for c in range(parts):
-            copy(h, l, e, c, 2).start()
-            copy(h, l, e, c, 3).start()
-        for t in range(high):
-            from_core(t, 1 - l)
-
+    swapped(1)
+
+    def follow(t):
+        @pl.when(h == t)
+        def _():
+            own_z(1, 0)
+
+        @pl.when(h + t == high - 1)
+        def _():
+            own_z(1, 1)
+
+    follow(0)
+    for t in range(1, high):
+        stage(0, t)
+        follow(t)
+        from_across(0, t - 1)
+    stage(1, 0)
+    stage(1, 1, y=False)
+    from_across(0, high - 1)
+    stage(1, 1, z=False)
+    from_core(0)
     tile = 512
 
     def pick(a):
         @pl.loop(0, pairs)
         def _(hp):
             for n in range(0, width, tile):
-                tokens = every[a, pl.ds(2 * hp, 2), :, :, pl.ds(n, tile)].reshape(tokens_here, tile)
+                tokens = every[a, pl.ds(2 * hp, 2), :, :, :, pl.ds(n, tile)].reshape(tokens_here, tile)
                 value = jnp.dot(choose_ref[a, hp], tokens, preferred_element_type=jnp.float32)
                 for i in range(experts):
                     picked[i, hp, :, pl.ds(n, tile)] = value[i * slots : (i + 1) * slots].astype(
@@ -712,56 +739,63 @@
                 ).astype(picked.dtype)
                 picked[i, :, :, pl.ds(n, tile)] = value.reshape(pairs, slots, tile)
             for k, hook in hooks:
-                @pl.when((e == 1) & (i == min(k, experts - 1)))
+                @pl.when(i == min(k, experts - 1))
                 def _():
                     hook()
             return carry
 
         lax.fori_loop(0, experts, run, 0)
 
-    order = []
-    for i in range(high):
-        order.append(i // 2 if i % 2 == 0 else high - 1 - i // 2)
-    turns = []
-    for h0 in order:
-        if h0 // 2 not in turns:
-            turns.append(h0 // 2)
-    shape = (2,) + every.shape[2:4]
-
-    def to_near(h0, l0, c):
-        at = pl.ds(c * rows, rows)
-        return pltpu.make_async_remote_copy(
-            src_ref=every.at[1 - e, h0, l0, at],
-            dst_ref=near.at[h0, l0, at],
-            send_sem=near_s.at[h0, l0, c],
-            recv_sem=near_r.at[h0, l0, c],
+    turns = [jnp.where(2 * h >= high, k, pairs - 1 - k) for k in range(pairs)]
+
+    def far_first(act_on):
+        for d in range(high - 1, -1, -1):
+            for _, h0, fits in at_distance(d):
+                @pl.when(fits)
+                def _():
+                    act_on(h0)
+
+    shape = (2,) + every.shape[2:5]
+
+    def to_near(a, h0, l0, j):
+        return pltpu.make_async_remote_copy(
+            src_ref=every.at[a, h0, l0, theirs[j]],
+            dst_ref=near.at[a, h0, l0, j],
+            send_sem=near_s.at[a, h0, l0, j],
+            recv_sem=near_r.at[a, h0, l0, j],
             device_id={"exp": 1 - e},
             device_id_type=mesh_id,
         )
 
-    def to_across(h0, c):
-        at = pl.ds(c * rows, rows)
-        return pltpu.make_async_remote_copy(
-            src_ref=sums.at[h0, at],
-            dst_ref=across.at[h0, at],
-            send_sem=across_s.at[h0, c],
-            recv_sem=across_r.at[h0, c],
+    def to_across(a, h0, j):
+        return pltpu.make_async_remote_copy(
+            src_ref=sums.at[a, h0, j],
+            dst_ref=across.at[a, h0, j],
+            send_sem=across_s.at[a, h0, j],
+            recv_sem=across_r.at[a, h0, j],
             device_id={"seq": h * LOW + 1 - l},
             device_id_type=mesh_id,
         )
 
-    def to_line(way, h0, c):
-        at = pl.ds(c * rows, rows)
-        return pltpu.make_async_remote_copy(
-            src_ref=running.at[h0, at],
-            dst_ref=line.at[way, h0, at],
-            send_sem=line_s.at[way, h0, c],
-            recv_sem=line_r.at[way, h0, c],
+    def to_line(way, a, h0, j):
+        return pltpu.make_async_remote_copy(
+            src_ref=running.at[a, h0, j],
+            dst_ref=line.at[way, a, h0, j],
+            send_sem=line_s.at[way, a, h0, j],
+            recv_sem=line_r.at[way, a, h0, j],
             device_id={"seq": (h - 1 + 2 * way) * LOW + l},
             device_id_type=mesh_id,
         )
 
-    pieces = [(h0, c) for h0 in order for c in range(parts)]
+    def to_other(j):
+        return pltpu.make_async_remote_copy(
+            src_ref=ours.at[j],
+            dst_ref=given.at[j],
+            send_sem=last_s.at[j],
+            recv_sem=last_r.at[j],
+            device_id={"exp": 1 - e},
+            device_id_type=mesh_id,
+        )
 
     def combine(a):
         for hp in turns:
@@ -770,152 +804,153 @@
                     [picked[i, hp, :, pl.ds(n, tile)] for i in range(experts)], axis=0
                 )
                 value = jnp.dot(combine_ref[a, hp], rows_here, preferred_element_type=jnp.float32)
-                every[a, 2 * hp : 2 * hp + 2, :, :, pl.ds(n, tile)] = value.astype(every.dtype).reshape(
-                    shape + (tile,)
-                )
-
-            @pl.when(e != a)
+                every[a, pl.ds(2 * hp, 2), :, :, :, pl.ds(n, tile)] = value.astype(
+                    every.dtype
+                ).reshape(shape + (tile,))
+            for l0 in (1 - l, l):
+                for h0 in (2 * hp, 2 * hp + 1):
+                    for j in range(half):
+                        to_near(a, h0, l0, j).start()
+
+    def pair_sum(a, h0, l0, j):
+        return every[a, h0, l0, mine[j]].astype(jnp.float32) + near[a, h0, l0, j].astype(jnp.float32)
+
+    def over_y(a):
+        def one(h0):
+            for j in range(half):
+                to_near(a, h0, 1 - l, j).wait_recv()
+                sums[a, h0, j] = pair_sum(a, h0, 1 - l, j).astype(sums.dtype)
+                to_across(a, h0, j).start()
+
+        far_first(one)
+
+    def held(a, h0, j):
+        return pair_sum(a, h0, l, j) + across[a, h0, j].astype(jnp.float32)
+
+    def ready(a, h0, j):
+        to_near(a, h0, l, j).wait_recv()
+        to_across(a, h0, j).wait_recv()
+
+    def hand_on(a, h0, j):
+        ready(a, h0, j)
+        for way, fits, first_here in ((0, h0 < h, h + 1 >= high), (1, h0 > h, h <= 0)):
+            @pl.when(fits)
             def _():
-                for l0 in (1 - l, l):
-                    for h0 in (2 * hp, 2 * hp + 1):
-                        for c in range(parts):
-                            to_near(h0, l0, c).start()
-
-    def over_y():
-        for h0, c in pieces:
-            at = pl.ds(c * rows, rows)
-            to_near(h0, 1 - l, c).wait_recv()
-            value = every[e, h0, 1 - l, at].astype(jnp.float32) + near[h0, 1 - l, at].astype(jnp.float32)
-            sums[h0, at] = value.astype(sums.dtype)
-            to_across(h0, c).start()
-
-    def along_line():
-        for h0, c in pieces:
-            at = pl.ds(c * rows, rows)
-            to_near(h0, l, c).wait_recv()
-            to_across(h0, c).wait_recv()
-
-            def held():
-                value = every[e, h0, l, at].astype(jnp.float32) + near[h0, l, at].astype(jnp.float32)
-                return value + across[h0, at].astype(jnp.float32)
-
-            @pl.when(h0 < h)
+                @pl.when(jnp.logical_not(first_here))
+                def _():
+                    to_line(way, a, h0, j).wait_recv()
+                    running[a, h0, j] = (
+                        held(a, h0, j) + line[way, a, h0, j].astype(jnp.float32)
+                    ).astype(running.dtype)
+
+                @pl.when(first_here)
+                def _():
+                    running[a, h0, j] = held(a, h0, j).astype(running.dtype)
+
+                to_line(way, a, h0, j).start()
+
+    def wave(a, k):
+        def one(h0):
+            @pl.when(((h0 < h) & (h + k == high - 1)) | ((h0 > h) & (h == k)))
             def _():
-                @pl.when(h + 1 < high)
-                def _():
-                    to_line(0, h0, c).wait_recv()
-                    running[h0, at] = (held() + line[0, h0, at].astype(jnp.float32)).astype(running.dtype)
-
-                @pl.when(h + 1 >= high)
-                def _():
-                    running[h0, at] = held().astype(running.dtype)
-
-                to_line(0, h0, c).start()
-
-            @pl.when(h0 > h)
-            def _():
-                @pl.when(h > 0)
-                def _():
-                    to_line(1, h0, c).wait_recv()
-                    running[h0, at] = (held() + line[1, h0, at].astype(jnp.float32)).astype(running.dtype)
-
-                @pl.when(h <= 0)
-                def _():
-                    running[h0, at] = held().astype(running.dtype)
-
-                to_line(1, h0, c).start()
+                for j in range(half):
+                    hand_on(a, h0, j)
+
+        far_first(one)
+
+    def arrived(a, j):
+        value = held(a, h, j)
+
+        @pl.when(h + 1 < high)
+        def _():
+            to_line(0, a, h, j).wait_recv()
+
+        @pl.when(h + 1 >= high)
+        def _():
+            line[0, a, h, j] = jnp.zeros_like(line[0, a, h, j])
+
+        @pl.when(h > 0)
+        def _():
+            to_line(1, a, h, j).wait_recv()
+
+        @pl.when(h <= 0)
+        def _():
+            line[1, a, h, j] = jnp.zeros_like(line[1, a, h, j])
+
+        return value + line[0, a, h, j].astype(jnp.float32) + line[1, a, h, j].astype(jnp.float32)
 
     pick(0)
     for one in loads:
         one.wait()
-    last = [(max(0, experts - 2), functools.partial(stage, t)) for t in range(3, high)]
-    run_experts(
-        [(0, functools.partial(stage, 1)), (0, functools.partial(from_across, 0))]
-        + [(1, functools.partial(stage, 2))] * (high > 2)
-        + last
-        + [(2, functools.partial(from_across, 1))] * (high > 1)
-    )
-
-    @pl.when(e == 0)
-    def _():
-        sent()
-
-    @pl.when(e == 1)
-    def _():
-        for t in range(2, high - 1):
-            from_across(t)
-
+    def later():
+        for t in range(3, high):
+            stage(1, t)
+
+    hooks = [(0, functools.partial(stage, 1, 2))] if high > 2 else []
+    hooks += [(1, functools.partial(from_across, 1, 0)), (2, later), (2, functools.partial(from_across, 1, 1))]
+    run_experts(hooks)
+    for t in range(2, high - 1):
+        from_across(1, t)
+    sent(0)
     combine(0)
     for hp in range(pairs):
         build(1, hp)
-
-    @pl.when(e == 1)
-    def _():
-        for t in range(max(2, high - 1), high):
-            from_across(t)
-
-    @pl.when(e == 0)
-    def _():
-        over_y()
-        for l0 in (l, 1 - l):
-            for t in range(high):
-                from_core(t, l0)
-
+    for t in range(max(2, high - 1), high):
+        from_across(1, t)
+    over_y(0)
+    from_core(1)
     pick(1)
     run_experts([])
-
-    @pl.when(e == 1)
-    def _():
-        sent()
-
+    sent(1)
     combine(1)
-
-    @pl.when(e == 1)
-    def _():
-        over_y()
-
-    along_line()
-    for c in range(parts):
-        at = pl.ds(c * rows, rows)
-        value = every[e, h, l, at].astype(jnp.float32) + near[h, l, at].astype(jnp.float32)
-        partial = value + across[h, at].astype(jnp.float32) + mixed_ref[at, :]
-
-        @pl.when(h + 1 < high)
-        def _():
-            to_line(0, h, c).wait_recv()
-
-        @pl.when(h + 1 >= high)
-        def _():
-            line[0, h, at] = jnp.zeros_like(line[0, h, at])
-
-        @pl.when(h > 0)
-        def _():
-            to_line(1, h, c).wait_recv()
-
-        @pl.when(h <= 0)
-        def _():
-            line[1, h, at] = jnp.zeros_like(line[1, h, at])
-
-        value = partial + line[0, h, at].astype(jnp.float32) + line[1, h, at].astype(jnp.float32)
-        out_ref[at, :] = value.astype(out_ref.dtype)
-
-    for h0, c in pieces:
-        for l0 in range(LOW):
-            to_near(h0, l0, c).wait_send()
-        to_across(h0, c).wait_send()
-
-        @pl.when(h0 < h)
-        def _():
-            to_line(0, h0, c).wait_send()
-
-        @pl.when(h0 > h)
-        def _():
-            to_line(1, h0, c).wait_send()
+    wave(0, 0)
+    over_y(1)
+    for k in range(1, high - 1):
+        wave(0, k)
+
+    def pass_on(h0):
+        for j in range(half):
+            hand_on(1, h0, j)
+
+    far_first(pass_on)
+    for j in range(half):
+        ready(0, h, j)
+    for j in range(half):
+        ours[j] = arrived(1 - e, j).astype(ours.dtype)
+        to_other(j).start()
+
+    def rows_of(c):
+        return pl.ds(pl.multiple_of(c * rows, rows), rows)
+
+    for j in range(half):
+        at = rows_of(mine[j])
+        out_ref[at, :] = (arrived(e, j) + mixed_ref[at, :]).astype(out_ref.dtype)
+    for j in range(half):
+        at = rows_of(theirs[j])
+        to_other(j).wait_recv()
+        out_ref[at, :] = (given[j].astype(jnp.float32) + mixed_ref[at, :]).astype(out_ref.dtype)
+    for a in range(2):
+        for h0 in range(high):
+            for j in range(half):
+                for l0 in range(LOW):
+                    to_near(a, h0, l0, j).wait_send()
+                to_across(a, h0, j).wait_send()
+
+                @pl.when(h0 < h)
+                def _():
+                    to_line(0, a, h0, j).wait_send()
+
+                @pl.when(h0 > h)
+                def _():
+                    to_line(1, a, h0, j).wait_send()
+    for j in range(half):
+        to_other(j).wait_send()
 
 
 def back(normed, mixed, meta, expert_in, expert_out, high, top):
     rows, width = mixed.shape
     parts = PARTS
+    half, piece = parts // 2, rows // parts
     whole = pl.BlockSpec(memory_space=pltpu.VMEM)
     away = pl.BlockSpec(memory_space=pl.ANY)
     kind = jnp.bfloat16
@@ -925,31 +960,34 @@
     tokens = LOW * 2 * rows
     pairs = high // 2
     return pl.pallas_call(
-        functools.partial(back_kernel, high, parts, top),
+        functools.partial(back_kernel, high, top),
         out_shape=jax.ShapeDtypeStruct((rows, width), kind),
         in_specs=[whole] * 3 + [away] * 2,
         out_specs=whole,
         scratch_shapes=[
             pltpu.VMEM((2, pairs, experts * slots, tokens), kind),
             pltpu.VMEM((2, pairs, tokens, experts * slots), kind),
-            pltpu.VMEM((2, high, LOW, rows, width), kind),
+            pltpu.VMEM((2, high, LOW, parts, piece, width), kind),
             pltpu.VMEM(expert_in.shape, kind),
             pltpu.VMEM(expert_out.shape, kind),
             pltpu.VMEM((experts, pairs, slots, width), kind),
             pltpu.VMEM((pairs * slots, expert_out.shape[1]), kind),
-            pltpu.VMEM((high, LOW, rows, width), kind),
-            pltpu.VMEM((high, rows, width), kind),
-            pltpu.VMEM((high, rows, width), kind),
-            pltpu.VMEM((high, rows, width), kind),
-            pltpu.VMEM((2, high, rows, width), kind),
-            sem((1,)),
+            pltpu.VMEM((2, high, LOW, half, piece, width), kind),
+            pltpu.VMEM((2, high, half, piece, width), kind),
+            pltpu.VMEM((2, high, half, piece, width), kind),
+            pltpu.VMEM((2, high, half, piece, width), kind),
+            pltpu.VMEM((2, 2, high, half, piece, width), kind),
+            pltpu.VMEM((half, piece, width), kind),
+            pltpu.VMEM((half, piece, width), kind),
+            sem((parts,)),
             sem((2, experts)),
-            sem((high, LOW, 2, parts)),
-            sem((4, high, LOW, parts)),
+            sem((2, high, LOW, parts)),
+            sem((4, 2, high, LOW, parts)),
         ]
-        + [sem((high, LOW, parts))] * 2
-        + [sem((high, parts))] * 2
-        + [sem((2, high, parts))] * 2,
+        + [sem((2, high, LOW, half))] * 2
+        + [sem((2, high, half))] * 2
+        + [sem((2, 2, high, half))] * 2
+        + [sem((half,))] * 2,
         compiler_params=pltpu.CompilerParams(
             collective_id=2, has_side_effects=True, vmem_limit_bytes=VMEM_LIMIT
         ),

time: 131 us -> 124 us (0.947); the launches traced: 131 us -> 122 us
  Pallas kernels: 130 us -> 120 us
    pallas_call x1, Pallas kernels: 78.8 us -> 69.6 us  [back(): pl.pallas_call(functools.partial(back_kernel, high, top), out_shape=jax.S...]
where the time goes in v3:
time: 124 us; the launch traced here: 122 us
  Pallas kernels  120 us (97%)
  local copies, waits for them, and re-layouts  1.67 us (1%)
    pallas_call x1, Pallas kernels, back(): pl.pallas_call(functools.partial(back_kernel, high, top), out_shape=jax.S...  69.6 us
    pallas_call x1, Pallas kernels, front(): pl.pallas_call(functools.partial(front_kernel, high, groups, chunks), out...  50.7 us

profile of v3, /device:TPU:9, one launch (start us, length us, event | category | flops | bytes accessed | tf_op | source)
XLA Modules:
  0.0 122.0 jit_solution(3949108822332306265)
XLA Ops:
  0.0 50.7 %front.1 = (f32[64,2048]{1,0:T(8,128)}, bf16[64,2048]{1,0:T(8,128)(2,1)}, bf16[4,2,2,16,128]{4,3,2,1,0:T(8,128)(2,1)}) custom-call(bf16[128,256]{1,0:T(8,128)(2,1)} %key_in.1, bf16[128,256]{1,0:T(8,128)(2,1)} %value_in.1, s32[8,64]{1,0:T(8,128)} %bitcast.4, f32[8,64]{1,0:T(8,128)} %bitcast.5, bf16[128,2048]{1,0:T(8,128)(2,1)} %query_in.1, ...), custom_call_target="tpu_custom_call" | custom-call | tf_op jit(solution)/shard_map/front/pallas_call | solution.py:485
  50.7 69.6 %back.1 = bf16[64,2048]{1,0:T(8,128)(2,1)} custom-call(bf16[64,2048]{1,0:T(8,128)(2,1)} %get-tuple-element.8.normed_ref, f32[64,2048]{1,0:T(8,128)} %get-tuple-element.9.mixed_ref, bf16[4,2,2,16,128]{4,3,2,1,0:T(8,128)(2,1)} %get-tuple-element.10.meta_ref, bf16[4,2048,1536]{2,1,0:T(8,128)(2,1)} %first_hbm.1, bf16[4,768,2048]{2,1,0:T(8,128)(2,1)} %second_hbm.1), custom_call_target="tpu_custom_call" | custom-call | tf_op jit(solution)/shard_map/back/pallas_call | solution.py:962
  120.3 1.7 %copy.12 = bf16[64,2048]{1,0:T(8,128)(2,1)} copy(bf16[64,2048]{1,0:T(8,128)(2,1)} %back.1) | data formatting | bytes 524288
